TPU v7x, 512 devices: a whole 4x4x16 slice. The times are simulated.
512 devices in a mesh: ctx: 64 (over y, z), head: 8 (over x, core).
Axes of the slice: x: 4, y: 4, z: 16, core: 2. Of those that a mesh axis runs over, the one named last changes fastest.
Arguments:
- queries: bfloat16 [4096, 32, 128], P(('ctx', 'head')), may hold values from -12 to 12
- fresh_keys: bfloat16 [4096, 8, 128], P(('ctx', 'head')), may hold values from -12 to 12
- fresh_values: bfloat16 [4096, 8, 128], P(('ctx', 'head')), may hold values from -6 to 6
- cache_keys: bfloat16 [262144, 8, 128], P('ctx', 'head'), may hold values from -12 to 12
- cache_values: bfloat16 [262144, 8, 128], P('ctx', 'head'), may hold values from -6 to 6
- selected: int32 [32, 12], replicated, may hold values from 0 to 63, all different within a row; in each aligned block of 32 rows (0 to 31, 32 to 63, ...) at most 6 rows name the same one
- start: int32 [1], replicated, may hold values from 253953 to 262144
Outputs:
- attended: bfloat16 [4096, 32, 128], P(('ctx', 'head'))
Inputs may be any that keep to these rules, and one draw needn't show every extreme that they name: Row t lists 12 different blocks selected by query tile t; no block is listed by more than 6 tiles, and some block by exactly 6.
All inputs are finite; a program needn't handle non-finite values.
Results may differ from a plain program's by a relative error of at most 0.0033.
Values may be sent and summed in bfloat16 or wider, within the bound.
No kernel may reach another device: no remote copies, remote signals or barrier semaphores. Data moves between devices by JAX's collectives and lax.ppermute only.
A program may use at most 128 MiB of HBM per device.

v0:
```python
import jax
import jax.numpy as jnp
from jax import lax
from jax.sharding import PartitionSpec as P

TILE = 128


masked_score = -1e30


def attend_piece(running, query_rows, key_block, value_block, allowed):
    old_max, old_total, old_sum = running
    scale = key_block.shape[-1] ** (-0.5)
    scores = (
        jnp.einsum("tkgd,nkd->kgtn", query_rows, key_block, preferred_element_type=jnp.float32)
        * scale
    )
    scores = jnp.where(allowed[None, None], scores, masked_score)
    new_max = jnp.maximum(old_max, jnp.max(scores, axis=-1))
    weights = jnp.where(allowed[None, None], jnp.exp(scores - new_max[..., None]), 0.0)
    shrink = jnp.exp(old_max - new_max)
    totals = old_total * shrink + jnp.sum(weights, axis=-1)
    product = jnp.einsum(
        "kgtn,nkd->kgtd",
        weights.astype(jnp.bfloat16),
        value_block,
        preferred_element_type=jnp.float32,
    )
    return (new_max, totals, old_sum * shrink[..., None] + product)


def shards(queries, fresh_keys, fresh_values, cache_keys, cache_values, selected, start):
    queries_here, keys_here, values_here = (
        lax.all_to_all(queries, "head", split_axis=1, concat_axis=0, tiled=True),
        lax.all_to_all(fresh_keys, "head", split_axis=1, concat_axis=0, tiled=True),
        lax.all_to_all(fresh_values, "head", split_axis=1, concat_axis=0, tiled=True),
    )
    q_count = queries_here.shape[0]
    q_heads = queries_here.shape[1]
    kv_heads = keys_here.shape[1]
    head_size = queries_here.shape[2]
    per_group = q_heads // kv_heads
    ctx_size = lax.axis_size("ctx")
    ctx_index = lax.axis_index("ctx")
    query_rows = queries_here.reshape(q_count, kv_heads, per_group, head_size)
    query_pos = ctx_index * q_count + jnp.arange(q_count, dtype=jnp.int32)
    initial = (
        jnp.full((kv_heads, per_group, q_count), masked_score, jnp.float32),
        jnp.zeros((kv_heads, per_group, q_count), jnp.float32),
        jnp.zeros((kv_heads, per_group, q_count, head_size), jnp.float32),
    )
    key_block = lax.all_gather(keys_here, "ctx", axis=0, tiled=True)
    value_block = lax.all_gather(values_here, "ctx", axis=0, tiled=True)
    key_pos = jnp.arange(key_block.shape[0], dtype=jnp.int32)
    allowed = key_pos[None, :] <= query_pos[:, None]
    own_max, own_total, own_sum = attend_piece(initial, query_rows, key_block, value_block, allowed)
    block_len = cache_keys.shape[0]
    sub_len = min(block_len, 1024)
    sub_count = block_len // sub_len
    tile_count = selected.shape[0]
    sel_count = selected.shape[1]
    per_tile = TILE // q_count
    capacity = min(max(2, q_count * sel_count // TILE), tile_count)
    wanted = jnp.any(selected == ctx_index, axis=1).astype(jnp.int32)
    ranking = jnp.cumsum(wanted) - 1
    slot_ids = jnp.arange(capacity, dtype=jnp.int32)
    chosen = (wanted[None, :] == 1) & (ranking[None, :] == slot_ids[:, None])
    tile_ids = jnp.sum(
        jnp.where(chosen, jnp.arange(tile_count, dtype=jnp.int32)[None, :], 0), axis=1
    )
    is_live = jnp.any(chosen, axis=1)
    sources = (
        tile_ids[:, None] * per_tile + jnp.arange(per_tile, dtype=jnp.int32)[None, :]
    ).reshape(-1)
    targets = jnp.where(jnp.repeat(is_live, per_tile), sources, ctx_size)
    limit = start[0]
    query_flat = queries_here.reshape(q_count, q_heads * head_size)
    query_slots = jnp.broadcast_to(query_flat[None], (ctx_size, q_count, q_heads * head_size))
    received = lax.all_to_all(query_slots, "ctx", split_axis=0, concat_axis=0, tiled=True)
    item_count = received.shape[1]
    picked = jnp.take(received, jnp.minimum(sources, ctx_size - 1), axis=0)
    picked = picked.reshape(capacity, per_tile * item_count, kv_heads, per_group, head_size)

    def one_tile(tile_rows):
        tile_len = tile_rows.shape[0]
        start_state = (
            jnp.full((kv_heads, per_group, tile_len), masked_score, jnp.float32),
            jnp.zeros((kv_heads, per_group, tile_len), jnp.float32),
            jnp.zeros((kv_heads, per_group, tile_len, head_size), jnp.float32),
        )

        def advance(state, sub_index):
            key_block = lax.dynamic_slice_in_dim(cache_keys, sub_index * sub_len, sub_len, 0)
            value_block = lax.dynamic_slice_in_dim(cache_values, sub_index * sub_len, sub_len, 0)
            cache_pos = (
                ctx_index * block_len + sub_index * sub_len + jnp.arange(sub_len, dtype=jnp.int32)
            )
            allowed = (cache_pos < limit)[None, :]
            return (attend_piece(state, tile_rows, key_block, value_block, allowed), None)

        final_state, _ = lax.scan(advance, start_state, jnp.arange(sub_count, dtype=jnp.int32))
        return final_state

    tile_max, tile_total, tile_sum = lax.map(one_tile, picked)
    tile_max = jnp.transpose(
        tile_max.reshape(capacity, kv_heads, per_group, per_tile, item_count), (0, 3, 4, 1, 2)
    )
    tile_max = tile_max.reshape(capacity * per_tile, item_count, q_heads)
    tile_total = jnp.transpose(
        tile_total.reshape(capacity, kv_heads, per_group, per_tile, item_count), (0, 3, 4, 1, 2)
    )
    tile_total = tile_total.reshape(capacity * per_tile, item_count, q_heads)
    tile_sum = tile_sum.reshape(capacity, kv_heads, per_group, per_tile, item_count, head_size)
    tile_sum = jnp.transpose(tile_sum, (0, 3, 4, 1, 2, 5)).reshape(
        capacity * per_tile, item_count, q_heads * head_size
    )
    max_slots = (
        jnp.full((ctx_size, item_count, q_heads), masked_score, jnp.float32)
        .at[targets]
        .set(tile_max, mode="drop")
    )
    total_slots = (
        jnp.zeros((ctx_size, item_count, q_heads), jnp.float32)
        .at[targets]
        .set(tile_total, mode="drop")
    )
    sum_slots = (
        jnp.zeros((ctx_size, item_count, q_heads * head_size), jnp.float32)
        .at[targets]
        .set(tile_sum, mode="drop")
    )
    back_sum = lax.all_to_all(sum_slots, "ctx", split_axis=0, concat_axis=0, tiled=True)
    back_max = lax.all_to_all(max_slots, "ctx", split_axis=0, concat_axis=0, tiled=True)
    back_total = lax.all_to_all(total_slots, "ctx", split_axis=0, concat_axis=0, tiled=True)
    own_max = jnp.transpose(own_max, (2, 0, 1)).reshape(q_count, q_heads)
    own_total = jnp.transpose(own_total, (2, 0, 1)).reshape(q_count, q_heads)
    own_sum = jnp.transpose(own_sum, (2, 0, 1, 3)).reshape(q_count, q_heads, head_size)
    row_max = jnp.maximum(own_max, jnp.max(back_max, axis=0))
    own_scale = jnp.exp(own_max - row_max)
    back_scale = jnp.exp(back_max - row_max[None])
    back_sum = back_sum.reshape(ctx_size, q_count, q_heads, head_size)
    numerator = own_sum * own_scale[..., None] + jnp.sum(back_sum * back_scale[..., None], axis=0)
    denominator = own_total * own_scale + jnp.sum(back_total * back_scale, axis=0)
    result = (numerator / denominator[..., None]).astype(jnp.bfloat16)
    return lax.all_to_all(result, "head", split_axis=0, concat_axis=1, tiled=True)


def solution(mesh):
    in_specs = (
        P(("ctx", "head"), None, None),
        P(("ctx", "head"), None, None),
        P(("ctx", "head"), None, None),
        P("ctx", "head", None),
        P("ctx", "head", None),
        P(),
        P(),
    )
    out_specs = P(("ctx", "head"), None, None)
    return jax.shard_map(shards, mesh=mesh, in_specs=in_specs, out_specs=out_specs, check_vma=False)
```

profile of v0, /device:TPU:1, one launch (start us, length us, event | category | flops | bytes accessed | tf_op | source)
XLA Modules:
  0.0 855.1 jit_solution(2910093073210934034)
XLA Ops:
  7.4 14.1 %all_to_all.89 = bf16[8,32,128]{2,0,1:T(8,128)(2,1)S(1)} all-to-all(bf16[8,32,128]{2,0,1:T(8,128)(2,1)S(1)} %copy.46), channel_id=1, replica_groups=mesh['ctx'=64,'head'=8] {'head'}, dimensions={1} | all-to-all | bytes 131072 | tf_op jit(solution)/shard_map/all_to_all | solution.py:35
  21.5 2.5 broadcast_in_dim.165
  23.9 15.2 %all-to-all-start.3 = ((bf16[64,64,512]{2,1,0:T(8,128)(2,1)}), bf16[64,64,512]{2,1,0:T(8,128)(2,1)}, u32[]{:S(2)}, u32[]{:S(2)}) async-start(bf16[64,64,512]{2,1,0:T(8,128)(2,1)} %broadcast_in_dim.165), calls=%async_computation.3 | async-start | bytes 8388608 | tf_op jit(solution)/shard_map/all_to_all | solution.py:80
  41.5 181.6 %all-to-all-done.3 = bf16[64,64,512]{2,1,0:T(8,128)(2,1)} async-done(((bf16[64,64,512]{2,1,0:T(8,128)(2,1)}), bf16[64,64,512]{2,1,0:T(8,128)(2,1)}, u32[]{:S(2)}, u32[]{:S(2)}) %all-to-all-start.3) | async-done | bytes 4194336 | tf_op jit(solution)/shard_map/all_to_all | solution.py:80
  223.1 8.1 all-to-all-start
  231.3 2.8 gather_fusion
  235.9 4.6 all-to-all-start.2
  240.5 152.6 %while.42 = (s32[]{:T(128)}, f32[6,1,4,128]{3,2,1,0:T(4,128)S(1)}, f32[6,1,4,128]{3,2,1,0:T(4,128)S(1)}, f32[6,1,4,128,128]{4,3,2,1,0:T(8,128)}, bf16[6,128,1,4,...) while((s32[]{:T(128)}, f32[6,1,4,128]{3,2,1,0:T(4,128)S(1)}, ...), condition=%wide.region_10.11_spmd, body=%wide.region_5.0_spmd.sunk | while | flops 275452928 | bytes 8566296 | solution.py:105
  240.6 24.6 %while.43 = (s32[]{:T(128)}, f32[1,4,128]{2,1,0:T(4,128)S(1)}, f32[1,4,128]{2,1,0:T(4,128)S(1)}, f32[1,4,128,128]{3,2,1,0:T(8,128)S(1)}, s32[4]{0:T(128)S(1)}, /...) while((s32[]{:T(128)}, f32[1,4,128]{2,1,0:T(4,128)S(1)}, ...), condition=%wide.region_9.9_spmd.clone, body=%wide.region_6.8_spmd.clone.sunk | while | flops 275452928 | bytes 7509231 | solution.py:102
  242.5 1.4 bitcast_reduce_fusion.3
  244.8 2.0 fusion.79
  248.6 1.4 bitcast_reduce_fusion.3
  250.9 2.0 fusion.79
  257.1 2.0 fusion.79
  260.9 1.4 bitcast_reduce_fusion.3
  263.2 2.0 fusion.79
  266.0 24.6 %while.43 = (s32[]{:T(128)}, f32[1,4,128]{2,1,0:T(4,128)S(1)}, f32[1,4,128]{2,1,0:T(4,128)S(1)}, f32[1,4,128,128]{3,2,1,0:T(8,128)S(1)}, s32[4]{0:T(128)S(1)}, /...) while((s32[]{:T(128)}, f32[1,4,128]{2,1,0:T(4,128)S(1)}, ...), condition=%wide.region_9.9_spmd.clone, body=%wide.region_6.8_spmd.clone.sunk | while | flops 275452928 | bytes 7509231 | solution.py:102
  270.2 2.0 fusion.79
  274.0 1.4 bitcast_reduce_fusion.3
  276.4 2.0 fusion.79
  282.5 2.0 fusion.79
  286.3 1.4 bitcast_reduce_fusion.3
  288.7 2.0 fusion.79
  291.5 24.6 %while.43 = (s32[]{:T(128)}, f32[1,4,128]{2,1,0:T(4,128)S(1)}, f32[1,4,128]{2,1,0:T(4,128)S(1)}, f32[1,4,128,128]{3,2,1,0:T(8,128)S(1)}, s32[4]{0:T(128)S(1)}, /...) while((s32[]{:T(128)}, f32[1,4,128]{2,1,0:T(4,128)S(1)}, ...), condition=%wide.region_9.9_spmd.clone, body=%wide.region_6.8_spmd.clone.sunk | while | flops 275452928 | bytes 7509231 | solution.py:102
  293.3 1.4 bitcast_reduce_fusion.3
  295.6 2.0 fusion.79
  301.8 2.0 fusion.79
  305.6 1.4 bitcast_reduce_fusion.3
  307.9 2.0 fusion.79
  314.1 2.0 fusion.79
  316.9 24.6 %while.43 = (s32[]{:T(128)}, f32[1,4,128]{2,1,0:T(4,128)S(1)}, f32[1,4,128]{2,1,0:T(4,128)S(1)}, f32[1,4,128,128]{3,2,1,0:T(8,128)S(1)}, s32[4]{0:T(128)S(1)}, /...) while((s32[]{:T(128)}, f32[1,4,128]{2,1,0:T(4,128)S(1)}, ...), condition=%wide.region_9.9_spmd.clone, body=%wide.region_6.8_spmd.clone.sunk | while | flops 275452928 | bytes 7509231 | solution.py:102
  318.7 1.4 bitcast_reduce_fusion.3
  321.1 2.0 fusion.79
  327.2 2.0 fusion.79
  333.3 2.0 fusion.79
  339.5 2.0 fusion.79
  342.3 24.6 %while.43 = (s32[]{:T(128)}, f32[1,4,128]{2,1,0:T(4,128)S(1)}, f32[1,4,128]{2,1,0:T(4,128)S(1)}, f32[1,4,128,128]{3,2,1,0:T(8,128)S(1)}, s32[4]{0:T(128)S(1)}, /...) while((s32[]{:T(128)}, f32[1,4,128]{2,1,0:T(4,128)S(1)}, ...), condition=%wide.region_9.9_spmd.clone, body=%wide.region_6.8_spmd.clone.sunk | while | flops 275452928 | bytes 7509231 | solution.py:102
  344.2 1.4 bitcast_reduce_fusion.3
  346.5 2.0 fusion.79
  352.6 2.0 fusion.79
  358.8 2.0 fusion.79
  364.9 2.0 fusion.79
  367.7 24.6 %while.43 = (s32[]{:T(128)}, f32[1,4,128]{2,1,0:T(4,128)S(1)}, f32[1,4,128]{2,1,0:T(4,128)S(1)}, f32[1,4,128,128]{3,2,1,0:T(8,128)S(1)}, s32[4]{0:T(128)S(1)}, /...) while((s32[]{:T(128)}, f32[1,4,128]{2,1,0:T(4,128)S(1)}, ...), condition=%wide.region_9.9_spmd.clone, body=%wide.region_6.8_spmd.clone.sunk | while | flops 275452928 | bytes 7509231 | solution.py:102
  371.9 2.0 fusion.79
  378.0 2.0 fusion.79
  384.2 2.0 fusion.79
  390.3 2.0 fusion.79
  394.9 7.2 all-to-all-start.4
  403.9 11.7 %all-to-all-done.4 = f32[64,1,256]{2,1,0:T(1,128)S(1)} async-done(((f32[64,1,256]{2,1,0:T(1,128)}), f32[64,1,256]{2,1,0:T(1,128)S(1)}, u32[]{:S(2)}, u32[]{:S(2)}) %all-to-all-start.4) | async-done | bytes 65568 | tf_op jit(solution)/shard_map/all_to_all | solution.py:134
  415.6 5.5 all-to-all-start.6
  421.2 2.4 copy.71
  424.3 4.3 broadcast_in_dim.167
  428.6 3.4 scatter_fusion.1
  432.0 2.7 all-to-all-done.6
  434.7 12.2 %all-to-all-start.5 = ((f32[64,64,512]{2,1,0:T(8,128)}), f32[64,64,512]{2,1,0:T(8,128)}, u32[]{:S(2)}, u32[]{:S(2)}) async-start(f32[64,64,512]{2,1,0:T(8,128)} %scatter_fusion.1), calls=%async_computation.5 | async-start | bytes 16777216 | tf_op jit(solution)/shard_map/all_to_all | solution.py:133
  448.3 174.4 %all-gather.3.cloned.1.call-done = bf16[4096,1,128]{2,0,1:T(8,128)(2,1)} async-done(((bf16[64,1,128]{2,0,1:T(8,128)(2,1)}), bf16[4096,1,128]{2,0,1:T(8,128)(2,1)}) %all-gather.3.cloned.1.call-update) | async-done | bytes 1048592 | tf_op jit(solution)/shard_map/all_gather | solution.py:53
  622.7 2.2 fusion.68
  624.9 2.0 copy-done
  631.2 7.1 mul.112
  638.3 10.3 %mul.113 = f32[64,64,512]{2,1,0:T(8,128)} reshape(f32[64,64,4,128]{3,2,1,0:T(4,128)} %mul.112) | data formatting | bytes 16777216 | tf_op jit(solution)/shard_map/mul | solution.py:143
  648.6 177.5 %all-to-all-done.5 = f32[64,64,512]{2,1,0:T(8,128)} async-done(((f32[64,64,512]{2,1,0:T(8,128)}), f32[64,64,512]{2,1,0:T(8,128)}, u32[]{:S(2)}, u32[]{:S(2)}) %all-to-all-start.5) | async-done | bytes 8388640 | tf_op jit(solution)/shard_map/all_to_all | solution.py:133
  826.1 7.6 multiply_reduce_fusion
  833.7 3.4 fusion.50
  837.2 10.4 %all_to_all.90 = bf16[64,4,128]{2,1,0:T(4,128)(2,1)S(1)} all-to-all(bf16[64,4,128]{2,1,0:T(4,128)(2,1)S(1)} %copy.56), channel_id=1, replica_groups=mesh['ctx'=64,'head'=8] {'head'}, dimensions={0} | all-to-all | bytes 131072 | tf_op jit(solution)/shard_map/all_to_all | solution.py:146
  (277 shorter events, 93.2 us)
Async XLA Ops:
  23.9 15.3 %copy-start.3 = (bf16[8,8,128]{2,1,0:T(8,128)(2,1)S(1)}, bf16[8,8,128]{2,1,0:T(8,128)(2,1)}, u32[]{:S(2)}) copy-start(bf16[8,8,128]{2,1,0:T(8,128)(2,1)} %param.12) | copy-start | bytes 49156
  23.9 15.9 %copy-start.4 = (bf16[8,8,128]{2,1,0:T(8,128)(2,1)S(1)}, bf16[8,8,128]{2,1,0:T(8,128)(2,1)}, u32[]{:S(2)}) copy-start(bf16[8,8,128]{2,1,0:T(8,128)(2,1)} %param.13) | copy-start | bytes 49156
  23.9 16.5 %copy-start.5 = (s32[32,12]{0,1:T(8,128)S(1)}, s32[32,12]{0,1:T(8,128)}, u32[]{:S(2)}) copy-start(s32[32,12]{0,1:T(8,128)} %param.16) | copy-start | bytes 4612
  23.9 199.2 %all-to-all-start.3 = ((bf16[64,64,512]{2,1,0:T(8,128)(2,1)}), bf16[64,64,512]{2,1,0:T(8,128)(2,1)}, u32[]{:S(2)}, u32[]{:S(2)}) async-start(bf16[64,64,512]{2,1,0:T(8,128)(2,1)} %broadcast_in_dim.165), calls=%async_computation.3 | async-start | bytes 8388608 | tf_op jit(solution)/shard_map/all_to_all | solution.py:80
  223.1 12.8 %all-to-all-start = ((bf16[8,8,128]{2,0,1:T(8,128)(2,1)}), bf16[8,8,128]{2,0,1:T(8,128)(2,1)S(1)}, u32[]{:S(2)}, u32[]{:S(2)}) async-start(bf16[8,8,128]{2,0,1:T(8,128)(2,1)} %copy.45), calls=%async_computation | async-start | bytes 32768 | tf_op jit(solution)/shard_map/all_to_all | solution.py:36
  235.9 4.6 copy-start.2
  235.9 159.0 %all-to-all-start.2 = ((bf16[8,8,128]{2,0,1:T(8,128)(2,1)}), bf16[8,8,128]{2,0,1:T(8,128)(2,1)S(1)}, u32[]{:S(2)}, u32[]{:S(2)}) async-start(bf16[8,8,128]{2,0,1:T(8,128)(2,1)} %copy.48), calls=%async_computation.2 | async-start | bytes 32768 | tf_op jit(solution)/shard_map/all_to_all | solution.py:37
  394.9 28.7 %copy-start.1 = (bf16[8,8,128]{2,0,1:T(8,128)(2,1)}, bf16[8,8,128]{2,0,1:T(8,128)(2,1)S(1)}, u32[]{:S(2)}) copy-start(bf16[8,8,128]{2,0,1:T(8,128)(2,1)S(1)} %all-to-all-done.2) | copy-start | bytes 49156
  394.9 20.7 %all-to-all-start.4 = ((f32[64,1,256]{2,1,0:T(1,128)}), f32[64,1,256]{2,1,0:T(1,128)S(1)}, u32[]{:S(2)}, u32[]{:S(2)}) async-start(f32[64,1,256]{2,1,0:T(1,128)} %reshape.400), calls=%async_computation.4 | async-start | bytes 131072 | tf_op jit(solution)/shard_map/all_to_all | solution.py:134
  415.6 19.0 %all-to-all-start.6 = ((f32[64,1,256]{2,1,0:T(1,128)}), f32[64,1,256]{2,1,0:T(1,128)S(1)}, u32[]{:S(2)}, u32[]{:S(2)}) async-start(f32[64,1,256]{2,1,0:T(1,128)} %reshape.402), calls=%async_computation.6 | async-start | bytes 131072 | tf_op jit(solution)/shard_map/all_to_all | solution.py:135
  434.7 391.4 %all-to-all-start.5 = ((f32[64,64,512]{2,1,0:T(8,128)}), f32[64,64,512]{2,1,0:T(8,128)}, u32[]{:S(2)}, u32[]{:S(2)}) async-start(f32[64,64,512]{2,1,0:T(8,128)} %scatter_fusion.1), calls=%async_computation.5 | async-start | bytes 16777216 | tf_op jit(solution)/shard_map/all_to_all | solution.py:133
  446.9 175.9 %all-gather.3.cloned.1.call-start = ((), (), s32[]{:S(2)}) async-start(), calls=%async_computation.8 | async-start | bytes 1064960 | tf_op jit(solution)/shard_map/all_gather | solution.py:53
  447.6 386.1 %all-gather.5.cloned.1.call-start = ((), (), s32[]{:S(2)}) async-start(), calls=%async_computation.9 | async-start | bytes 1064960 | tf_op jit(solution)/shard_map/all_gather | solution.py:54
  624.9 2.1 copy-start
Sparse Core Ops, SparseCore 0:
  450.6 172.0 all-gather.2
  625.7 178.9 all-gather.4
where the time goes:
time: 858 us; the launch traced here: 855 us
  waiting for transfers between devices  549 us (64%)
  matrix products  86.4 us (10%)
  local copies, waits for them, and re-layouts  63.1 us (7%)
  starting transfers between devices  53.1 us (6%)
  other arithmetic  49.9 us (6%)
  blocking collectives  24.5 us (3%)
  loops' own time  15.4 us (2%)
  between operations  13.7 us (2%)
    all_to_all x1, waiting for transfers between devices, shards(): lax.all_to_all(query_slots, 'ctx', split_axis=0, concat_axis=0, tiled=True)  182 us
    all_to_all x1, waiting for transfers between devices, shards(): lax.all_to_all(sum_slots, 'ctx', split_axis=0, concat_axis=0, tiled=True)  177 us
    all_gather x1, waiting for transfers between devices, shards(): key_block = lax.all_gather(keys_here, 'ctx', axis=0, tiled=True)  174 us
    dot_general x25, matrix products, attend_piece(): jnp.einsum('kgtn,nkd->kgtd', weights.astype(jnp.bfloat16), value_block, p...  50.4 us
    dot_general x25, matrix products, attend_piece(): jnp.einsum('tkgd,nkd->kgtn', query_rows, key_block, preferred_element_typ...  36 us
    reduce_sum x25, other arithmetic, attend_piece(): totals = old_total * shrink + jnp.sum(weights, axis=-1)  21.9 us
    mul x2, local copies, waits for them, and re-layouts, shards(): back_sum * back_scale[..., None]  17.4 us
  transfers between devices with their start and end apart: 8, of which 6 were waited for; matrix products, arithmetic and copies ran while one was open for 22% of the time, Pallas kernels for 0%

commit v1 on v0

v1 whole, which is shorter than its diff:
```python
import functools
import math

import jax
import jax.numpy as jnp
from jax import lax
from jax.experimental import pallas as pl
from jax.experimental.pallas import tpu as pltpu
from jax.sharding import PartitionSpec as P

TILE = 128
CHUNKS = 2
KEYS = 512
NEG = -1e30


def plan_kernel(tiles, sel, capacity, me_ref, sel_ref, tile_ref, index_ref, own_ref, count_ref):
    me, per_tile = me_ref[0], me_ref[1]

    def clear(b, _):
        count_ref[b] = 0
        return 0

    lax.fori_loop(0, count_ref.shape[0], clear, 0)
    for i in range(capacity):
        tile_ref[i] = 0

    own_tile = me // per_tile

    def one_tile(t, _):
        hit = jnp.int32(-1)
        for k in range(sel):
            b = sel_ref[t, k]
            slot = jnp.minimum(count_ref[b], capacity - 1)
            count_ref[b] = count_ref[b] + 1
            hit = jnp.where(b == me, slot, hit)
            own_ref[k] = jnp.where(t == own_tile, b * capacity + slot, own_ref[k])
            index_ref[tiles * sel + k] = b * capacity + slot

        @pl.when(hit >= 0)
        def _():
            tile_ref[hit] = t
            for k in range(sel):
                index_ref[hit * sel + k] = index_ref[tiles * sel + k]

        return 0

    for k in range(sel):
        own_ref[k] = 0
    lax.fori_loop(0, tiles, one_tile, 0)


def plan(selected, ctx_index, per_tile, capacity, blocks):
    tiles, sel = selected.shape
    smem = pl.BlockSpec(memory_space=pltpu.SMEM)
    tile_ids, index, own = pl.pallas_call(
        functools.partial(plan_kernel, tiles, sel, capacity),
        out_shape=(
            jax.ShapeDtypeStruct((capacity,), jnp.int32),
            jax.ShapeDtypeStruct(((tiles + 1) * sel,), jnp.int32),
            jax.ShapeDtypeStruct((sel,), jnp.int32),
        ),
        in_specs=[smem, smem],
        out_specs=(smem, smem, smem),
        scratch_shapes=[pltpu.SMEM((blocks,), jnp.int32)],
        name="plan",
    )(jnp.stack([ctx_index, jnp.int32(per_tile)]), selected)
    return tile_ids, index, own


def column_to_row(column):
    return jnp.broadcast_to(column, (column.shape[0], 128)).T[0:1, :]


def row_to_columns(row):
    return jnp.broadcast_to(row, (128, row.shape[1])).T


def keep(block, width, limit):
    return block * width + lax.broadcasted_iota(jnp.int32, (1, width), 1) < limit


def max_kernel(tile_ref, valid_ref, q_ref, kt_ref, wide_ref, row_ref):
    q = q_ref[0]
    rows = q.shape[0]
    length = kt_ref.shape[1]
    valid = valid_ref[0]

    def run(masked):
        best = None
        for j in range(length // KEYS):
            s = jnp.dot(q, kt_ref[:, j * KEYS : (j + 1) * KEYS], preferred_element_type=jnp.float32)
            if masked:
                s = jnp.where(keep(j, KEYS, valid), s, NEG)
            for g in range(KEYS // 128):
                part = s[:, g * 128 : (g + 1) * 128]
                best = part if best is None else jnp.maximum(best, part)
        top = jnp.max(best, axis=1, keepdims=True)
        wide_ref[0] = jnp.broadcast_to(top, (rows, 128))
        row_ref[0] = column_to_row(top)

    pl.when(valid == length)(lambda: run(False))
    pl.when(valid != length)(lambda: run(True))


def block_max(tile_ids, valid, q, kt):
    capacity = tile_ids.shape[0]
    rows = q.shape[1]
    return pl.pallas_call(
        max_kernel,
        out_shape=(
            jax.ShapeDtypeStruct((capacity, rows, 128), jnp.float32),
            jax.ShapeDtypeStruct((capacity, 1, rows), jnp.float32),
        ),
        grid_spec=pltpu.PrefetchScalarGridSpec(
            num_scalar_prefetch=2,
            grid=(capacity,),
            in_specs=[
                pl.BlockSpec((1, rows, 128), lambda i, t, v: (t[i], 0, 0)),
                pl.BlockSpec(kt.shape, lambda i, t, v: (0, 0)),
            ],
            out_specs=(
                pl.BlockSpec((1, rows, 128), lambda i, t, v: (i, 0, 0)),
                pl.BlockSpec((1, 1, rows), lambda i, t, v: (i, 0, 0)),
            ),
        ),
        name="block_max",
    )(tile_ids, valid, q, kt)


def gathered_max(stats_ref, index_ref, first, sel):
    best = stats_ref[pl.ds(index_ref[first], 1), :]
    for k in range(1, sel):
        best = jnp.maximum(best, stats_ref[pl.ds(index_ref[first + k], 1), :])
    return best


def sum_kernel(
    factor, sel, tile_ref, valid_ref, index_ref, q_ref, kt_ref, v_ref, wide_ref, stats_ref, zero_ref, out_ref
):
    del zero_ref
    i = pl.program_id(0)
    q = q_ref[0]
    rows = q.shape[0]
    length = kt_ref.shape[1]
    valid = valid_ref[0]
    half = rows // 2
    row_top = gathered_max(stats_ref, index_ref, i * sel, sel)

    def run(masked):
        top = wide_ref[0]
        tops = jnp.concatenate([top] * (KEYS // 128), axis=1)
        total = jnp.zeros((rows, 128), jnp.float32)
        acc = jnp.zeros((rows, 128), jnp.float32)
        for j in range(length // KEYS):
            s = jnp.dot(q, kt_ref[:, j * KEYS : (j + 1) * KEYS], preferred_element_type=jnp.float32)
            p = jnp.exp2((s - tops) * factor)
            if masked:
                p = jnp.where(keep(j, KEYS, valid), p, 0.0)
            for g in range(KEYS // 128):
                total += p[:, g * 128 : (g + 1) * 128]
            acc += jnp.dot(
                p.astype(jnp.bfloat16),
                v_ref[j * KEYS : (j + 1) * KEYS, :],
                preferred_element_type=jnp.float32,
            )
        shrink = jnp.exp2((top - row_to_columns(row_top)) * factor)
        acc = acc * shrink
        sums = column_to_row(jnp.sum(total, axis=1, keepdims=True) * shrink[:, 0:1])
        for side in range(2):
            out_ref[0, side, 0:half, :] = acc[side * half : (side + 1) * half]
            out_ref[0, side, half : half + 8, :] = jnp.broadcast_to(
                sums[:, side * half : (side + 1) * half], (8, half)
            )

    pl.when(valid == length)(lambda: run(False))
    pl.when(valid != length)(lambda: run(True))


def block_sum(factor, tile_ids, valid, index, q, kt, v, wide, stats, zeros):
    capacity = tile_ids.shape[0]
    rows = q.shape[1]
    sel = index.shape[0] // (q.shape[0] + 1)
    return pl.pallas_call(
        functools.partial(sum_kernel, factor, sel),
        out_shape=jax.ShapeDtypeStruct(zeros.shape, jnp.float32),
        grid_spec=pltpu.PrefetchScalarGridSpec(
            num_scalar_prefetch=3,
            grid=(capacity,),
            in_specs=[
                pl.BlockSpec((1, rows, 128), lambda i, t, v, x: (t[i], 0, 0)),
                pl.BlockSpec(kt.shape, lambda i, t, v, x: (0, 0)),
                pl.BlockSpec(v.shape, lambda i, t, v, x: (0, 0)),
                pl.BlockSpec((1, rows, 128), lambda i, t, v, x: (i, 0, 0)),
                pl.BlockSpec(stats.shape, lambda i, t, v, x: (0, 0)),
                pl.BlockSpec(memory_space=pl.ANY),
            ],
            out_specs=pl.BlockSpec((1,) + zeros.shape[1:], lambda i, t, v, x: (t[i], 0, 0, 0)),
        ),
        input_output_aliases={8: 0},
        name="block_sum",
    )(tile_ids, valid, index, q, kt, v, wide, stats, zeros)


def fresh_kernel(factor, tokens, me_ref, q_ref, k_ref, v_ref, acc_ref, top_ref, total_ref, s_ref):
    rows = q_ref.shape[0]
    first = me_ref[0] * tokens
    steps = (first + tokens + KEYS - 1) // KEYS
    position = first + lax.rem(lax.broadcasted_iota(jnp.int32, (rows, KEYS), 0), tokens)
    column = lax.broadcasted_iota(jnp.int32, (rows, KEYS), 1)
    top_ref[...] = jnp.full((rows, 128), NEG, jnp.float32)

    def score(j, _):
        key = k_ref[pl.ds(pl.multiple_of(j * KEYS, KEYS), KEYS), :]
        s = lax.dot_general(
            q_ref[...], key, (((1,), (1,)), ((), ())), preferred_element_type=jnp.float32
        )
        s = jnp.where(column + j * KEYS <= position, s, NEG)
        s_ref[j] = s
        best = top_ref[...]
        for g in range(KEYS // 128):
            best = jnp.maximum(best, s[:, g * 128 : (g + 1) * 128])
        top_ref[...] = best
        return 0

    lax.fori_loop(0, steps, score, 0)
    top_ref[...] = jnp.broadcast_to(jnp.max(top_ref[...], axis=1, keepdims=True), (rows, 128))
    acc_ref[...] = jnp.zeros((rows, 128), jnp.float32)
    total_ref[...] = jnp.zeros((rows, 128), jnp.float32)

    def weigh(j, _):
        tops = jnp.concatenate([top_ref[...]] * (KEYS // 128), axis=1)
        p = jnp.exp2((s_ref[j] - tops) * factor)
        total = total_ref[...]
        for g in range(KEYS // 128):
            total += p[:, g * 128 : (g + 1) * 128]
        total_ref[...] = total
        acc_ref[...] += jnp.dot(
            p.astype(jnp.bfloat16),
            v_ref[pl.ds(pl.multiple_of(j * KEYS, KEYS), KEYS), :],
            preferred_element_type=jnp.float32,
        )
        return 0

    lax.fori_loop(0, steps, weigh, 0)
    total_ref[...] = jnp.broadcast_to(jnp.sum(total_ref[...], axis=1, keepdims=True), (rows, 128))


def fresh_part(factor, tokens, me, q, k, v):
    rows = q.shape[0]
    wide = jax.ShapeDtypeStruct((rows, 128), jnp.float32)
    vmem = pl.BlockSpec(memory_space=pltpu.VMEM)
    return pl.pallas_call(
        functools.partial(fresh_kernel, factor, tokens),
        out_shape=(wide, wide, wide),
        in_specs=[pl.BlockSpec(memory_space=pltpu.SMEM), vmem, vmem, vmem],
        out_specs=(vmem, vmem, vmem),
        scratch_shapes=[pltpu.VMEM((k.shape[0] // KEYS, rows, KEYS), jnp.float32)],
        name="fresh_part",
    )(me, q, k, v)


def join_kernel(factor, sel, own_ref, side_ref, acc_ref, top_ref, total_ref, *refs):
    out_ref = refs[-1]
    chunks = (len(refs) - 1) // 2
    side = side_ref[0]
    for c in range(chunks):
        stats_ref, back_ref = refs[2 * c], refs[2 * c + 1]
        half = back_ref.shape[0] - 8
        row = gathered_max(stats_ref, own_ref, 0, sel)
        row = jnp.where(side == 0, row[:, 0:half], row[:, half : 2 * half])
        cache_top = row_to_columns(row)
        here = slice(c * half, (c + 1) * half)
        top = jnp.maximum(cache_top, top_ref[here, :])
        cache_scale = jnp.exp2((cache_top - top) * factor)
        own_scale = jnp.exp2((top_ref[here, :] - top) * factor)
        cache_total = row_to_columns(back_ref[half : half + 1, :])
        upper = acc_ref[here, :] * own_scale + back_ref[0:half, :] * cache_scale
        lower = total_ref[here, :] * own_scale + cache_total * cache_scale
        out_ref[here, :] = (upper / lower).astype(jnp.bfloat16)


def join(factor, own, side, acc, top, total, stats, back):
    vmem = pl.BlockSpec(memory_space=pltpu.VMEM)
    smem = pl.BlockSpec(memory_space=pltpu.SMEM)
    pairs = [x for pair in zip(stats, back) for x in pair]
    return pl.pallas_call(
        functools.partial(join_kernel, factor, own.shape[0]),
        out_shape=jax.ShapeDtypeStruct(acc.shape, jnp.bfloat16),
        in_specs=[smem, smem] + [vmem] * (3 + len(pairs)),
        out_specs=vmem,
        name="join",
    )(own, side, acc, top, total, *pairs)


def shards(queries, fresh_keys, fresh_values, cache_keys, cache_values, selected, start):
    part, q_heads, head_size = queries.shape
    kv_heads = fresh_keys.shape[1]
    group = q_heads // kv_heads
    heads_axis = lax.axis_size("head")
    ctx_size = lax.axis_size("ctx")
    ctx_index = lax.axis_index("ctx")
    tokens = part * heads_axis
    per_tile = TILE // tokens
    tiles, sel = selected.shape
    blocks = ctx_size
    capacity = tiles * sel // blocks
    factor = head_size**-0.5 * math.log2(math.e)
    length = cache_keys.shape[0]

    mixed = jnp.concatenate(
        [
            queries.reshape(part, kv_heads, group, head_size),
            fresh_keys[:, :, None],
            fresh_values[:, :, None],
        ],
        axis=2,
    ).transpose(1, 2, 0, 3)
    mixed = lax.all_to_all(mixed, "head", split_axis=0, concat_axis=0, tiled=True)
    mixed = mixed.transpose(1, 0, 2, 3).reshape(group + 2, tokens, head_size)
    own_q = mixed[:group].reshape(group * tokens, head_size)

    rows = group * tokens // CHUNKS
    gathered = [
        lax.all_gather(own_q[c * rows : (c + 1) * rows], "ctx", axis=0, tiled=True).reshape(
            tiles, per_tile * rows, head_size
        )
        for c in range(CHUNKS)
    ]
    fresh = lax.all_gather(mixed[group:], "ctx", axis=1, tiled=False)
    fresh = fresh.reshape(2, ctx_size * tokens, head_size)

    kt = cache_keys[:, 0].T
    v = cache_values[:, 0]
    tile_ids, index, own = plan(selected, ctx_index, per_tile, capacity, blocks)
    valid = jnp.clip(start - ctx_index * length, 0, length)

    tops = [block_max(tile_ids, valid, q, kt) for q in gathered]
    stats = [
        lax.all_gather(row[:, 0], "ctx", axis=0, tiled=True) for _, row in tops
    ]
    back = []
    for c in range(CHUNKS):
        zeros = jnp.zeros((tiles, per_tile, rows + 8, head_size), jnp.float32)
        spread = block_sum(
            factor, tile_ids, valid, index, gathered[c], kt, v, tops[c][0], stats[c], zeros
        )
        spread = spread.reshape(ctx_size * (rows + 8), head_size)
        back.append(lax.psum_scatter(spread, "ctx", scatter_dimension=0, tiled=True))
    acc, top, total = fresh_part(factor, tokens, ctx_index.reshape(1), own_q, fresh[0], fresh[1])
    side = (ctx_index % per_tile).reshape(1)
    result = join(factor, own, side, acc, top, total, stats, back)
    result = result.reshape(group, heads_axis, part, head_size).transpose(1, 0, 2, 3)
    result = lax.all_to_all(result, "head", split_axis=0, concat_axis=0, tiled=True)
    return result.reshape(q_heads, part, head_size).transpose(1, 0, 2)


def solution(mesh):
    in_specs = (
        P(("ctx", "head"), None, None),
        P(("ctx", "head"), None, None),
        P(("ctx", "head"), None, None),
        P("ctx", "head", None),
        P("ctx", "head", None),
        P(),
        P(),
    )
    out_specs = P(("ctx", "head"), None, None)
    return jax.shard_map(shards, mesh=mesh, in_specs=in_specs, out_specs=out_specs, check_vma=False)
```

time: 858 us -> 1490 us (1.74)
  waiting for transfers between devices: 549 us -> 1220 us
  blocking collectives: 24.5 us -> 178 us
  matrix products: 86.4 us -> 0 us
  Pallas kernels: 0 us -> 55 us
  starting transfers between devices: 53.1 us -> 0.16 us
  other arithmetic: 49.9 us -> 0.63 us
  local copies, waits for them, and re-layouts: 63.1 us -> 17.5 us
  loops' own time: 15.4 us -> 0 us
    unnamed x2 -> x7, waiting for transfers between devices: 0.97 us -> 1020 us
    all_to_all x6 -> x0, waiting for transfers between devices: 374 us -> none  [the longest x1 182 us: shards(): lax.all_to_all(query_slots, 'ctx', split_axis=0, concat_axis=0, tiled=True)]
    all_gather x0 -> x2, blocking collectives: none -> 144 us  [shards(): lax.all_gather(row[:, 0], 'ctx', axis=0, tiled=True)]
    dot_general x50 -> x0, matrix products: 86.4 us -> none  [the longest x25 50.4 us: attend_piece(): jnp.einsum('kgtn,nkd->kgtd', weights.astype(jnp.bfloat16), value_block, p...]
    pallas_call x0 -> x7, Pallas kernels: none -> 55 us  [the longest x2 30 us: block_sum(): pl.pallas_call(functools.partial(sum_kernel, factor, sel), out_shape=jax....]
    all_to_all x6 -> x0, starting transfers between devices: 52.8 us -> none  [the longest x1 15.2 us: shards(): lax.all_to_all(query_slots, 'ctx', split_axis=0, concat_axis=0, tiled=True)]
    reduce_sum x28 -> x0, other arithmetic: 29.7 us -> none  [the longest x25 21.9 us: attend_piece(): totals = old_total * shrink + jnp.sum(weights, axis=-1)]
    all_gather x2 -> x3, waiting for transfers between devices: 174 us -> 203 us  [the longest x2 161 us: shards(): lax.all_gather(own_q[c * rows:(c + 1) * rows], 'ctx', axis=0, tiled=True)]
  transfers between devices with their start and end apart: 8 -> 5, of which waited for: 6 -> 5; matrix products, arithmetic and copies ran while one was open for 22% -> 1% of each run, Pallas kernels for 0% -> 4%
where the time goes in v1:
time: 1490 us
  waiting for transfers between devices  1220 us (82%)
  blocking collectives  178 us (12%)
  Pallas kernels  55 us (4%)
  local copies, waits for them, and re-layouts  17.5 us (1%)
    unnamed x7, waiting for transfers between devices  1020 us
    all_gather x2, waiting for transfers between devices, shards(): lax.all_gather(own_q[c * rows:(c + 1) * rows], 'ctx', axis=0, tiled=True)  161 us
    all_gather x2, blocking collectives, shards(): lax.all_gather(row[:, 0], 'ctx', axis=0, tiled=True)  144 us
    all_gather x1, waiting for transfers between devices, shards(): fresh = lax.all_gather(mixed[group:], 'ctx', axis=1, tiled=False)  41.7 us
    pallas_call x2, Pallas kernels, block_sum(): pl.pallas_call(functools.partial(sum_kernel, factor, sel), out_shape=jax....  30 us
  transfers between devices with their start and end apart: 5, of which 5 were waited for; matrix products, arithmetic and copies ran while one was open for 1% of the time, Pallas kernels for 4%

profile of v1, /device:TPU:1, one launch (start us, length us, event | category | flops | bytes accessed | tf_op | source)
XLA Modules:
  0.0 1486.5 jit_solution(11215929686004329605)
XLA Ops:
  6.5 0.0 all-gather.10.cloned.1.call-start
  6.5 0.9 copy.35
  7.4 0.7 copy_bitcast_fusion.5
  8.2 14.2 all_to_all.10
  22.4 0.6 fusion.1
  23.0 0.0 all-gather.10.cloned.1.call-update
  23.0 0.0 all-gather.8.cloned.1.call-start
  23.1 0.7 all-gather.8.cloned.1.call-update
  23.8 0.0 all-gather.6.cloned.1.call-start
  23.8 0.7 all-gather.6.cloned.1.call-update
  24.5 0.0 reduce-scatter.9.cloned.1.call-start
  24.6 1.4 copy.34.sel_ref
  26.6 2.3 copy.39
  28.9 0.6 pad_add_fusion.me_ref
  29.6 4.6 plan.1
  34.2 119.3 %all-gather.10.cloned.1.call-done = bf16[8192,128]{1,0:T(8,128)(2,1)} async-done(((bf16[128,128]{1,0:T(8,128)(2,1)}), bf16[8192,128]{1,0:T(8,128)(2,1)}) %all-gather.10.cloned.1.call-update) | async-done | bytes 2097168 | tf_op jit(solution)/shard_map/all_gather | solution.py:325
  153.5 7.7 block_max.3
  161.2 72.0 %all-gather.1 = f32[384,1,256]{2,1,0:T(1,128)S(1)} all-gather(f32[6,1,256]{2,1,0:T(1,128)} %get-tuple-element.23), channel_id=3, replica_groups=mesh['ctx'=64,'head'=8] {'ctx'}, dimensions={0}, use_global_device_ids=true | all-gather | bytes 399360 | tf_op jit(solution)/shard_map/all_gather | solution.py:340
  233.2 0.8 copy.51
  234.0 2.4 broadcast_1_zero_ref.2.clone.1.zero_ref
  236.4 15.0 %block_sum.3 = f32[32,2,136,128]{3,2,1,0:T(8,128)} custom-call(s32[6]{0:T(128)} %get-tuple-element.19.tile_ref, s32[1]{0:T(128)S(6)} %min.6.valid_ref, s32[396]{0:T(512)} %get-tuple-element.21.index_ref, bf16[32,256,128]{2,1,0:T(8,128)(2,1)} %bitcast.52, bf16[128,4096]{1,0:T(8,128)(2,1)} %bitcast.46, ...), custom_call_target="tpu_custom_call", output_to_operand_aliasing={{}: (8, {})} | custom-call | tf_op jit(solution)/shard_map/block_sum/pallas_call | solution.py:184
  251.4 0.0 reduce-scatter.9.cloned.1.call-update
  251.4 0.0 reduce-scatter.7.cloned.1.call-start
  251.4 42.1 %all-gather.8.cloned.1.call-done = bf16[8192,128]{1,0:T(8,128)(2,1)} async-done(((bf16[128,128]{1,0:T(8,128)(2,1)}), bf16[8192,128]{1,0:T(8,128)(2,1)}) %all-gather.8.cloned.1.call-update) | async-done | bytes 2097168 | tf_op jit(solution)/shard_map/all_gather | solution.py:325
  293.5 7.7 block_max.2
  301.2 72.1 %all-gather = f32[384,1,256]{2,1,0:T(1,128)S(1)} all-gather(f32[6,1,256]{2,1,0:T(1,128)} %get-tuple-element.20), channel_id=2, replica_groups=mesh['ctx'=64,'head'=8] {'ctx'}, dimensions={0}, use_global_device_ids=true | all-gather | bytes 399360 | tf_op jit(solution)/shard_map/all_gather | solution.py:340
  373.3 0.8 copy.52
  374.1 2.3 broadcast_1_zero_ref.2.clone.zero_ref
  376.4 15.0 %block_sum.2 = f32[32,2,136,128]{3,2,1,0:T(8,128)} custom-call(s32[6]{0:T(128)} %get-tuple-element.19.tile_ref, s32[1]{0:T(128)S(6)} %min.6.valid_ref, s32[396]{0:T(512)} %get-tuple-element.21.index_ref, bf16[32,256,128]{2,1,0:T(8,128)(2,1)} %bitcast.50, bf16[128,4096]{1,0:T(8,128)(2,1)} %bitcast.48, ...), custom_call_target="tpu_custom_call", output_to_operand_aliasing={{}: (8, {})} | custom-call | tf_op jit(solution)/shard_map/block_sum/pallas_call | solution.py:184
  391.4 0.0 reduce-scatter.7.cloned.1.call-update
  391.4 0.6 slice.38
  392.1 41.7 %all-gather.6.cloned.1.call-done = bf16[2,64,64,128]{3,2,0,1:T(8,128)(2,1)} async-done(((bf16[2,1,64,128]{3,2,0,1:T(8,128)(2,1)}), bf16[2,64,64,128]{3,2,0,1:T(8,128)(2,1)}) %all-gather.6.cloned.1.call-update) | async-done | bytes 2097168 | tf_op jit(solution)/shard_map/all_gather | solution.py:330
  433.7 3.1 fusion
  436.9 2.9 fresh_part.1
  439.8 503.6 %reduce-scatter.9.cloned.1.call-done.refs_3_ = f32[136,128]{1,0:T(8,128)} async-done(((f32[8704,128]{1,0:T(8,128)}), f32[136,128]{1,0:T(8,128)}) %reduce-scatter.9.cloned.1.call-update) | async-done | bytes 69648
  943.4 513.1 %reduce-scatter.7.cloned.1.call-done.refs_1_ = f32[136,128]{1,0:T(8,128)} async-done(((f32[8704,128]{1,0:T(8,128)}), f32[136,128]{1,0:T(8,128)}) %reduce-scatter.7.cloned.1.call-update) | async-done | bytes 69648
  1456.5 2.1 join.1
  1458.6 0.9 copy.55
  1459.5 19.9 %all_to_all.11 = bf16[8,4,8,128]{3,2,1,0:T(8,128)(2,1)S(1)} all-to-all(bf16[8,4,8,128]{3,2,1,0:T(8,128)(2,1)S(1)} %bitcast.66), channel_id=1, replica_groups=mesh['ctx'=64,'head'=8] {'head'}, dimensions={0} | all-to-all | bytes 131072 | tf_op jit(solution)/shard_map/all_to_all | solution.py:354
  1479.3 0.6 copy.54
  (2 shorter events, 0.0 us)
Async XLA Ops:
  6.5 147.0 %all-gather.10.cloned.1.call-start = ((), (), s32[]{:S(2)}) async-start(), calls=%async_computation.6 | async-start | bytes 2129920 | tf_op jit(solution)/shard_map/all_gather | solution.py:325
  23.0 270.5 %all-gather.8.cloned.1.call-start = ((), (), s32[]{:S(2)}) async-start(), calls=%async_computation.5 | async-start | bytes 2129920 | tf_op jit(solution)/shard_map/all_gather | solution.py:325
  23.8 409.9 %all-gather.6.cloned.1.call-start = ((), (), s32[]{:S(2)}) async-start(), calls=%async_computation.4 | async-start | bytes 2129920 | tf_op jit(solution)/shard_map/all_gather | solution.py:330
  24.5 918.9 %reduce-scatter.9.cloned.1.call-start = ((), (), s32[]{:S(2)}) async-start(), calls=%async_computation.8 | async-start | bytes 4526080
  251.4 1205.1 %reduce-scatter.7.cloned.1.call-start = ((), (), s32[]{:S(2)}) async-start(), calls=%async_computation.7 | async-start | bytes 4526080
Sparse Core Ops, SparseCore 0:
  23.2 130.2 all-gather.9
  156.4 137.0 all-gather.7
  296.5 137.2 all-gather.5
  437.9 505.4 reduce-scatter.8
  947.6 508.8 reduce-scatter.6

commit v2 on v0

v2 whole, which is shorter than its diff:
```python
import functools
import math

import jax
import jax.numpy as jnp
from jax import lax
from jax.experimental import pallas as pl
from jax.experimental.pallas import tpu as pltpu
from jax.sharding import PartitionSpec as P

TILE = 128
RING = 16
KEYS = 512
NEG = -1e30
NONE = -4000.0
FINE = 2.0**19
FULL = 32767.0


def plan_kernel(ring, per_row, me_ref, sel_ref, tile_ref, flag_ref):
    tiles, sel = sel_ref.shape
    me = me_ref[0]
    y, z = me // ring, lax.rem(me, ring)
    for i in range(tile_ref.shape[0]):
        tile_ref[i] = 0
    for i in range(flag_ref.shape[0]):
        flag_ref[i] = 0

    def one_tile(t, count):
        hit = jnp.int32(0)
        mine = t // per_row == y
        for k in range(sel):
            b = sel_ref[t, k]
            hit = jnp.where(b == me, 1, hit)

            @pl.when(mine & (lax.rem(b, ring) == z))
            def _():
                flag_ref[(b // ring) * per_row + lax.rem(t, per_row)] = 1

        @pl.when(hit == 1)
        def _():
            tile_ref[jnp.minimum(count, tile_ref.shape[0] - 1)] = t

        return count + hit

    lax.fori_loop(0, tiles, one_tile, jnp.int32(0))


def plan(selected, me, ring, per_row, capacity, rows_of_chips):
    smem = pl.BlockSpec(memory_space=pltpu.SMEM)
    return pl.pallas_call(
        functools.partial(plan_kernel, ring, per_row),
        out_shape=(
            jax.ShapeDtypeStruct((capacity,), jnp.int32),
            jax.ShapeDtypeStruct((rows_of_chips * per_row,), jnp.int32),
        ),
        in_specs=[smem, smem],
        out_specs=(smem, smem),
        name="plan",
    )(me, selected)


def row_to_columns(row):
    return jnp.broadcast_to(row, (128, row.shape[1])).T


def pack(out_view, acc, level):
    rows = acc.shape[0]
    largest = jnp.maximum(jnp.max(jnp.abs(acc), axis=1, keepdims=True), 1e-30)
    code = jnp.round(acc * (FULL / largest)).astype(jnp.int32)
    out_view[0:rows, :] = code.astype(jnp.int16)
    lane = lax.broadcasted_iota(jnp.int32, (rows, 128), 1)
    both = jnp.where(lane == 0, level, jnp.log2(largest)).T[0:8, :]
    whole = jnp.round(jnp.clip(both, NONE, -NONE) * FINE).astype(jnp.int32)
    high = whole >> 16
    low = (whole & 0xFFFF) - 32768
    rank = lax.broadcasted_iota(jnp.int32, (8, 128), 0)
    stats = jnp.zeros((8, 128), jnp.int32)
    n = rows // 128
    for k, source in enumerate((high, low)):
        for stat in range(2):
            for g in range(n):
                piece = jnp.broadcast_to(source[stat : stat + 1, g * 128 : (g + 1) * 128], (8, 128))
                stats = jnp.where(rank == (k * 2 + stat) * n + g, piece, stats)
    out_view[rows : rows + 8, :] = stats.astype(jnp.int16)


def unpack_stats(view, rows):
    n = rows // 128
    raw = view[rows : rows + 8, :].astype(jnp.int32)
    found = []
    for stat in range(2):
        high = [raw[stat * n + g : stat * n + g + 1, :] for g in range(n)]
        low = [raw[(2 + stat) * n + g : (2 + stat) * n + g + 1, :] for g in range(n)]
        whole = [(h << 16) + (w + 32768) for h, w in zip(high, low)]
        found.append(jnp.concatenate([w.astype(jnp.float32) for w in whole], axis=1) * (1.0 / FINE))
    return found


def block_kernel(
    factor, tile_ref, valid_ref, q_ref, next_ref, kt_ref, v_ref, out_ref, s0_ref, s1_ref, top_ref, total_ref, acc_ref
):
    i = pl.program_id(0)
    length = kt_ref.shape[1]
    rows = q_ref.shape[3]
    valid = valid_ref[0]
    steps = length // KEYS

    def score(q, s_ref, slot, j):
        s = jnp.dot(q, kt_ref[:, j * KEYS : (j + 1) * KEYS], preferred_element_type=jnp.float32)
        position = lax.broadcasted_iota(jnp.int32, (1, KEYS), 1) + j * KEYS
        s = s + jnp.where(position < valid, 0.0, NEG)
        s_ref[:, j * KEYS : (j + 1) * KEYS] = s
        best = s[:, 0:128]
        for g in range(1, KEYS // 128):
            best = jnp.maximum(best, s[:, g * 128 : (g + 1) * 128])
        if j:
            best = jnp.maximum(best, top_ref[slot])
        if j == steps - 1:
            best = jnp.broadcast_to(jnp.max(best, axis=1, keepdims=True), (rows, 128))
        top_ref[slot] = best

    def weigh(s_ref, slot, j):
        tops = jnp.concatenate([top_ref[slot]] * (KEYS // 128), axis=1)
        p = jnp.exp2((s_ref[:, j * KEYS : (j + 1) * KEYS] - tops) * factor)
        total = p[:, 0:128]
        for g in range(1, KEYS // 128):
            total += p[:, g * 128 : (g + 1) * 128]
        product = jnp.dot(
            p.astype(jnp.bfloat16), v_ref[j * KEYS : (j + 1) * KEYS, :], preferred_element_type=jnp.float32
        )
        total_ref[...] = total_ref[...] + total if j else total
        acc_ref[...] = acc_ref[...] + product if j else product

    def finish(slot):
        total = jnp.sum(total_ref[...], axis=1, keepdims=True)
        level = top_ref[slot][:, 0:1] * factor + jnp.log2(total)
        level = jnp.where(valid > 0, level, NONE)
        pack(out_ref.at[0, 0, slot], acc_ref[...] / total, level)

    @pl.when(i == 0)
    def _():
        for j in range(steps):
            score(q_ref[0, 0, 0], s0_ref, 0, j)

    for j in range(steps):
        score(q_ref[0, 1, 0], s1_ref, 1, j)
        weigh(s0_ref, 0, j)
    finish(0)
    for j in range(steps):
        score(next_ref[0, 0, 0], s0_ref, 0, j)
        weigh(s1_ref, 1, j)
    finish(1)


def block_part(factor, tile_ids, valid, q, kt, v):
    per_row, sides, tile_rows, rows, _ = q.shape
    capacity = tile_ids.shape[0]
    return pl.pallas_call(
        functools.partial(block_kernel, factor),
        out_shape=jax.ShapeDtypeStruct((tile_rows, per_row, sides, rows + 8, 128), jnp.int16),
        grid_spec=pltpu.PrefetchScalarGridSpec(
            num_scalar_prefetch=2,
            grid=(capacity,),
            in_specs=[
                pl.BlockSpec(
                    (1, sides, 1, rows, 128),
                    lambda i, t, n: (lax.rem(t[i], per_row), 0, t[i] // per_row, 0, 0),
                ),
                pl.BlockSpec(
                    (1, 1, 1, rows, 128),
                    lambda i, t, n: (
                        lax.rem(t[jnp.minimum(i + 1, capacity - 1)], per_row),
                        0,
                        t[jnp.minimum(i + 1, capacity - 1)] // per_row,
                        0,
                        0,
                    ),
                ),
                pl.BlockSpec(kt.shape, lambda i, t, n: (0, 0)),
                pl.BlockSpec(v.shape, lambda i, t, n: (0, 0)),
            ],
            out_specs=pl.BlockSpec(
                (1, 1, sides, rows + 8, 128), lambda i, t, n: (t[i] // per_row, lax.rem(t[i], per_row), 0, 0, 0)
            ),
            scratch_shapes=[
                pltpu.VMEM((rows, kt.shape[1]), jnp.float32),
                pltpu.VMEM((rows, kt.shape[1]), jnp.float32),
                pltpu.VMEM((2, rows, 128), jnp.float32),
                pltpu.VMEM((rows, 128), jnp.float32),
                pltpu.VMEM((rows, 128), jnp.float32),
            ],
        ),
        name="block_part",
    )(tile_ids, valid, q, q, kt, v)


def column_kernel(factor, ring, tokens, flag_ref, me_ref, q_ref, k_ref, v_ref, got_ref, out_ref, acc_ref, top_ref, total_ref):
    k, side = pl.program_id(0), pl.program_id(1)
    per_row = pl.num_programs(0)
    y, z = me_ref[0], me_ref[1]
    rows = q_ref.shape[3]
    sources = got_ref.shape[0]
    keys = k_ref.shape[0]
    q = q_ref[0, 0, 0]
    s = lax.dot_general(q, k_ref[...], (((1,), (1,)), ((), ())), preferred_element_type=jnp.float32)
    row = lax.broadcasted_iota(jnp.int32, (rows, keys), 0)
    column = lax.broadcasted_iota(jnp.int32, (rows, keys), 1)
    here = (y * ring + k * (ring // per_row) + side) * tokens + lax.rem(row, tokens)
    there = (column // tokens * ring + z) * tokens + lax.rem(column, tokens)
    allowed = there <= here
    top = jnp.max(jnp.where(allowed, s, NEG), axis=1, keepdims=True)
    p = jnp.where(allowed, jnp.exp2((s - top) * factor), 0.0)
    high = p.astype(jnp.bfloat16)
    low = (p - high.astype(jnp.float32)).astype(jnp.bfloat16)
    acc_ref[...] = jnp.dot(high, v_ref[...], preferred_element_type=jnp.float32) + jnp.dot(
        low, v_ref[...], preferred_element_type=jnp.float32
    )
    total_ref[...] = jnp.broadcast_to(jnp.sum(p, axis=1, keepdims=True), (rows, 128))
    top_ref[...] = jnp.broadcast_to(jnp.maximum(top * factor, NONE), (rows, 128))
    for sy in range(sources):

        @pl.when(flag_ref[sy * per_row + k] == 1)
        def _():
            level, largest = unpack_stats(got_ref.at[sy, 0, 0], rows)
            level = row_to_columns(level)
            size = row_to_columns(jnp.exp2(largest) * (1.0 / FULL))
            old = top_ref[...]
            new = jnp.maximum(old, level)
            shrink = jnp.exp2(old - new)
            weight = jnp.exp2(level - new)
            value = got_ref[sy, 0, 0, 0:rows, :].astype(jnp.int32).astype(jnp.float32)
            acc_ref[...] = acc_ref[...] * shrink + value * (weight * size)
            total_ref[...] = total_ref[...] * shrink + weight
            top_ref[...] = new

    total = jnp.maximum(total_ref[...], 1e-30)
    level = jnp.maximum(top_ref[...] + jnp.log2(total), NONE)[:, 0:1]
    pack(out_ref.at[0], acc_ref[...] / total, level)


def column_part(factor, ring, tokens, flags, me, q, k, v, got):
    per_row, sides, tile_rows, rows, _ = q.shape
    sources = got.shape[0]
    return pl.pallas_call(
        functools.partial(column_kernel, factor, ring, tokens),
        out_shape=jax.ShapeDtypeStruct((per_row * sides, rows + 8, 128), jnp.int16),
        grid_spec=pltpu.PrefetchScalarGridSpec(
            num_scalar_prefetch=2,
            grid=(per_row, sides),
            in_specs=[
                pl.BlockSpec((1, 1, 1, rows, 128), lambda i, h, f, m: (i, h, m[0], 0, 0)),
                pl.BlockSpec(k.shape, lambda i, h, f, m: (0, 0)),
                pl.BlockSpec(v.shape, lambda i, h, f, m: (0, 0)),
                pl.BlockSpec((sources, 1, 1, rows + 8, 128), lambda i, h, f, m: (0, i, h, 0, 0)),
            ],
            out_specs=pl.BlockSpec((1, rows + 8, 128), lambda i, h, f, m: (i * sides + h, 0, 0)),
            scratch_shapes=[pltpu.VMEM((rows, 128), jnp.float32)] * 3,
        ),
        name="column_part",
    )(flags, me, q, k, v, got)


def ring_kernel(got_ref, out_ref):
    sources, padded, _ = got_ref.shape
    rows = padded - 8
    stats = [unpack_stats(got_ref.at[s], rows) for s in range(sources)]
    top = functools.reduce(jnp.maximum, [level for level, _ in stats])
    weights = [jnp.exp2(level - top) for level, _ in stats]
    total = functools.reduce(jnp.add, weights)
    acc = jnp.zeros((rows, 128), jnp.float32)
    for s in range(sources):
        share = row_to_columns(weights[s] * jnp.exp2(stats[s][1]) / (FULL * total))
        acc += got_ref[s, 0:rows, :].astype(jnp.int32).astype(jnp.float32) * share
    out_ref[...] = acc.astype(jnp.bfloat16)


def ring_part(got):
    vmem = pl.BlockSpec(memory_space=pltpu.VMEM)
    return pl.pallas_call(
        ring_kernel,
        out_shape=jax.ShapeDtypeStruct((got.shape[1] - 8, 128), jnp.bfloat16),
        in_specs=[vmem],
        out_specs=vmem,
        name="ring_part",
    )(got)


def shards(queries, fresh_keys, fresh_values, cache_keys, cache_values, selected, start):
    part, q_heads, head_size = queries.shape
    kv_heads = fresh_keys.shape[1]
    group = q_heads // kv_heads
    heads_axis = lax.axis_size("head")
    ctx_size = lax.axis_size("ctx")
    ctx_index = lax.axis_index("ctx")
    ring = RING
    columns = ctx_size // ring
    across = [[y * ring + z for y in range(columns)] for z in range(ring)]
    along = [[y * ring + z for z in range(ring)] for y in range(columns)]
    tokens = part * heads_axis
    sides = TILE // tokens
    per_row = ring // sides
    tiles, sel = selected.shape
    capacity = tiles * sel // ctx_size
    factor = head_size**-0.5 * math.log2(math.e)
    length = cache_keys.shape[0]
    rows = group * tokens

    mixed = jnp.concatenate(
        [
            queries.reshape(part, kv_heads, group, head_size),
            fresh_keys[:, :, None],
            fresh_values[:, :, None],
        ],
        axis=2,
    ).transpose(1, 2, 0, 3)
    mixed = lax.all_to_all(mixed, "head", split_axis=0, concat_axis=0, tiled=True)
    mixed = mixed.transpose(1, 0, 2, 3).reshape(group + 2, tokens, head_size)

    column = jnp.broadcast_to(mixed[None], (columns,) + mixed.shape)
    column = lax.all_to_all(
        column, "ctx", split_axis=0, concat_axis=0, tiled=True, axis_index_groups=across
    )
    column_q = column[:, :group].reshape(columns, rows, head_size)
    column_k = column[:, group].reshape(columns * tokens, head_size)
    column_v = column[:, group + 1].reshape(columns * tokens, head_size)
    q = lax.all_gather(column_q, "ctx", axis=0, tiled=True, axis_index_groups=along)
    q = q.reshape(per_row, sides, columns, rows, head_size)

    kt = cache_keys[:, 0].T
    v = cache_values[:, 0]
    tile_ids, flags = plan(selected, ctx_index.reshape(1), ring, per_row, capacity, columns)
    valid = jnp.clip(start - ctx_index * length, 0, length)

    sent = block_part(factor, tile_ids, valid, q, kt, v)
    got = lax.all_to_all(
        sent, "ctx", split_axis=0, concat_axis=0, tiled=True, axis_index_groups=across
    )
    me = jnp.stack([ctx_index // ring, ctx_index % ring])
    sent = column_part(factor, ring, tokens, flags, me, q, column_k, column_v, got)
    got = lax.all_to_all(
        sent, "ctx", split_axis=0, concat_axis=0, tiled=True, axis_index_groups=along
    )
    result = ring_part(got)
    result = result.reshape(group, heads_axis, part, head_size).transpose(1, 0, 2, 3)
    result = lax.all_to_all(result, "head", split_axis=0, concat_axis=0, tiled=True)
    return result.reshape(q_heads, part, head_size).transpose(1, 0, 2)


def solution(mesh):
    in_specs = (
        P(("ctx", "head"), None, None),
        P(("ctx", "head"), None, None),
        P(("ctx", "head"), None, None),
        P("ctx", "head", None),
        P("ctx", "head", None),
        P(),
        P(),
    )
    out_specs = P(("ctx", "head"), None, None)
    return jax.shard_map(shards, mesh=mesh, in_specs=in_specs, out_specs=out_specs, check_vma=False)
```

time: 858 us -> 275 us (0.32)
  waiting for transfers between devices: 549 us -> 100 us
  matrix products: 86.4 us -> 0 us
  blocking collectives: 24.5 us -> 97.1 us
  local copies, waits for them, and re-layouts: 63.1 us -> 8.21 us
  other arithmetic: 49.9 us -> 0.67 us
  Pallas kernels: 0 us -> 48.4 us
  starting transfers between devices: 53.1 us -> 4.85 us
  loops' own time: 15.4 us -> 0 us
    all_to_all x6 -> x1, waiting for transfers between devices: 374 us -> 39.6 us  [shards(): lax.all_to_all(sent, 'ctx', split_axis=0, concat_axis=0, tiled=True, axis...]
    all_gather x2 -> x1, waiting for transfers between devices: 174 us -> 60.4 us  [shards(): lax.all_gather(column_q, 'ctx', axis=0, tiled=True, axis_index_groups=along)]
    dot_general x50 -> x0, matrix products: 86.4 us -> none  [the longest x25 50.4 us: attend_piece(): jnp.einsum('kgtn,nkd->kgtd', weights.astype(jnp.bfloat16), value_block, p...]
    all_to_all x2 -> x4, blocking collectives: 24.5 us -> 97.1 us  [the longest x1 50.8 us: shards(): lax.all_to_all(sent, 'ctx', split_axis=0, concat_axis=0, tiled=True, axis...]
    pallas_call x0 -> x4, Pallas kernels: none -> 48.4 us  [the longest x1 23.6 us: block_part(): pl.pallas_call(functools.partial(block_kernel, factor), out_shape=jax.Sha...]
    all_to_all x6 -> x1, starting transfers between devices: 52.8 us -> 4.85 us  [shards(): lax.all_to_all(sent, 'ctx', split_axis=0, concat_axis=0, tiled=True, axis...]
    reduce_sum x28 -> x0, other arithmetic: 29.7 us -> none  [the longest x25 21.9 us: attend_piece(): totals = old_total * shrink + jnp.sum(weights, axis=-1)]
    mul x2 -> x0, local copies, waits for them, and re-layouts: 17.4 us -> none  [shards(): back_sum * back_scale[..., None]]
  transfers between devices with their start and end apart: 8 -> 2, of which waited for: 6 -> 2; matrix products, arithmetic and copies ran while one was open for 22% -> 2% of each run, Pallas kernels for 0% -> 2%
where the time goes in v2:
time: 275 us; the launch traced here: 273 us
  waiting for transfers between devices  100 us (36%)
  blocking collectives  97.1 us (35%)
  Pallas kernels  48.4 us (18%)
  between operations  14.1 us (5%)
  local copies, waits for them, and re-layouts  8.21 us (3%)
  starting transfers between devices  4.85 us (2%)
    all_gather x1, waiting for transfers between devices, shards(): lax.all_gather(column_q, 'ctx', axis=0, tiled=True, axis_index_groups=along)  60.4 us
    all_to_all x1, blocking collectives, shards(): lax.all_to_all(sent, 'ctx', split_axis=0, concat_axis=0, tiled=True, axis...  50.8 us
    all_to_all x1, waiting for transfers between devices, shards(): lax.all_to_all(sent, 'ctx', split_axis=0, concat_axis=0, tiled=True, axis...  39.6 us
    pallas_call x1, Pallas kernels, block_part(): pl.pallas_call(functools.partial(block_kernel, factor), out_shape=jax.Sha...  23.6 us
    all_to_all x1, blocking collectives, shards(): lax.all_to_all(result, 'head', split_axis=0, concat_axis=0, tiled=True)  22.6 us
    pallas_call x1, Pallas kernels, column_part(): pl.pallas_call(functools.partial(column_kernel, factor, ring, tokens), ou...  17.8 us
    all_to_all x1, blocking collectives, shards(): lax.all_to_all(mixed, 'head', split_axis=0, concat_axis=0, tiled=True)  14.2 us
    all_to_all x1, blocking collectives, shards(): lax.all_to_all(column, 'ctx', split_axis=0, concat_axis=0, tiled=True, ax...  9.5 us
  transfers between devices with their start and end apart: 2, of which 2 were waited for; matrix products, arithmetic and copies ran while one was open for 2% of the time, Pallas kernels for 2%

profile of v2, /device:TPU:1, one launch (start us, length us, event | category | flops | bytes accessed | tf_op | source)
XLA Modules:
  0.0 273.4 jit_solution(6639573817858252980)
XLA Ops:
  6.5 0.0 all-gather.2.cloned.1.call-start
  6.5 0.9 copy.26
  7.4 0.7 copy_bitcast_fusion.3
  8.2 14.2 %all_to_all.25 = bf16[8,6,8,128]{3,2,1,0:T(8,128)(2,1)S(1)} all-to-all(bf16[8,6,8,128]{3,2,1,0:T(8,128)(2,1)S(1)} %maximum_bitcast_fusion), channel_id=1, replica_groups=mesh['ctx'=64,'head'=8] {'head'}, dimensions={0} | all-to-all | bytes 196608 | tf_op jit(solution)/shard_map/all_to_all | solution.py:317
  22.4 0.1 broadcast_in_dim.16
  22.5 9.5 %all_to_all.26 = bf16[4,6,64,128]{3,2,1,0:T(8,128)(2,1)S(1)} all-to-all(bf16[4,6,64,128]{3,2,1,0:T(8,128)(2,1)S(1)} %broadcast_in_dim.16), channel_id=1, replica_groups={{0,128,256,384},{8,136,264,392},{16,144,272,400},{24,152,280,408},{32,1..., dimensions={0} | all-to-all | bytes 786432 | tf_op jit(solution)/shard_map/all_to_all | solution.py:321
  32.0 0.7 slice.12
  32.7 0.0 all-gather.2.cloned.1.call-update
  33.4 1.4 copy.25.sel_ref
  34.7 2.3 copy.30
  37.0 4.5 %plan.1 = (s32[6]{0:T(128)}, s32[32]{0:T(128)}) custom-call(s32[1]{0:T(128)} %bitcast.me_ref, s32[32,12]{1,0:T(8,128)} %copy.25.sel_ref), custom_call_target="tpu_custom_call" | custom-call | tf_op jit(solution)/shard_map/plan/pallas_call | solution.py:51
  41.5 60.4 %all-gather.2.cloned.1.call-done = bf16[64,256,128]{2,1,0:T(8,128)(2,1)} async-done(((bf16[4,256,128]{2,1,0:T(8,128)(2,1)}), bf16[64,256,128]{2,1,0:T(8,128)(2,1)}) %all-gather.2.cloned.1.call-update) | async-done | bytes 4194320 | tf_op jit(solution)/shard_map/all_gather | solution.py:327
  101.9 23.6 %block_part.1 = s16[4,8,2,264,128]{4,3,2,1,0:T(8,128)(2,1)} custom-call(s32[6]{0:T(128)} %get-tuple-element.8.tile_ref, s32[1]{0:T(128)S(6)} %min.6.valid_ref, bf16[8,2,4,256,128]{4,3,2,1,0:T(8,128)(2,1)} %bitcast.32, bf16[8,2,4,256,128]{4,3,2,1,0:T(8,128)(2,1)} %bitcast.33, bf16[128,4096]{1,0:T(8,128)(2,1)} %bitcast.35, bf16[4096,128]{1,0:T(8,128)(2,1)} %bitcast.36), custom_call_target="tpu_custom_call" | custom-call | tf_op jit(solution)/shard_map/block_part/pallas_call | solution.py:159
  125.5 4.9 %all-to-all-start.2 = ((s16[4,8,2,264,128]{4,3,2,1,0:T(8,128)(2,1)}), s16[4,8,2,264,128]{4,3,2,1,0:T(8,128)(2,1)}, u32[]{:S(2)}, u32[]{:S(2)}) async-start(s16[4,8,2,264,128]{4,3,2,1,0:T(8,128)(2,1)} %block_part.1), calls=%async_computation.2 | async-start | bytes 8650752 | tf_op jit(solution)/shard_map/all_to_all | solution.py:336
  130.4 0.7 pad_add_fusion.me_ref
  131.1 0.7 fusion
  131.7 39.6 %all-to-all-done.2.got_ref = s16[4,8,2,264,128]{4,3,2,1,0:T(8,128)(2,1)} async-done(((s16[4,8,2,264,128]{4,3,2,1,0:T(8,128)(2,1)}), s16[4,8,2,264,128]{4,3,2,1,0:T(8,128)(2,1)}, u32[]{:S(2)}, u32[]{:S(2)}) %all-to-all-start.2) | async-done | bytes 4325408 | tf_op jit(solution)/shard_map/all_to_all | solution.py:336
  171.3 17.8 %column_part.1 = s16[16,264,128]{2,1,0:T(8,128)(2,1)} custom-call(s32[32]{0:T(128)} %get-tuple-element.7.flag_ref, s32[2]{0:T(128)} %pad_add_fusion.me_ref, bf16[8,2,4,256,128]{4,3,2,1,0:T(8,128)(2,1)} %bitcast.34, bf16[256,128]{1,0:T(8,128)(2,1)} %bitcast.39, bf16[256,128]{1,0:T(8,128)(2,1)} %bitcast.38, s16[4,8,2,264,128]{4,3,2,1,0:T(8,128)(2,1)} %all-to-all-done.2.got_ref), custom_call_target="tpu_custom_call" | custom-call | tf_op jit(solution)/shard_map/column_part/pallas_call | solution.py:245
  189.1 50.8 %all_to_all.27.got_ref = s16[16,264,128]{2,1,0:T(8,128)(2,1)} all-to-all(s16[16,264,128]{2,1,0:T(8,128)(2,1)} %column_part.1), channel_id=1, replica_groups={{0,8,16,24,32,40,48,56,64,72,80,88,96,104,112,120},{128,136,144,152,160..., dimensions={0} | all-to-all | bytes 2162688 | tf_op jit(solution)/shard_map/all_to_all | solution.py:341
  239.9 2.5 ring_part.1
  242.5 0.9 copy.39
  243.3 22.6 %all_to_all.28 = bf16[8,4,8,128]{3,2,1,0:T(8,128)(2,1)S(1)} all-to-all(bf16[8,4,8,128]{3,2,1,0:T(8,128)(2,1)S(1)} %bitcast.42), channel_id=1, replica_groups=mesh['ctx'=64,'head'=8] {'head'}, dimensions={0} | all-to-all | bytes 131072 | tf_op jit(solution)/shard_map/all_to_all | solution.py:346
  266.0 0.6 copy.38
  (2 shorter events, 0.0 us)
Async XLA Ops:
  6.5 95.4 %all-gather.2.cloned.1.call-start = ((), (), s32[]{:S(2)}) async-start(), calls=%async_computation.5 | async-start | bytes 4456448 | tf_op jit(solution)/shard_map/all_gather | solution.py:327
  125.5 45.8 %all-to-all-start.2 = ((s16[4,8,2,264,128]{4,3,2,1,0:T(8,128)(2,1)}), s16[4,8,2,264,128]{4,3,2,1,0:T(8,128)(2,1)}, u32[]{:S(2)}, u32[]{:S(2)}) async-start(s16[4,8,2,264,128]{4,3,2,1,0:T(8,128)(2,1)} %block_part.1), calls=%async_computation.2 | async-start | bytes 8650752 | tf_op jit(solution)/shard_map/all_to_all | solution.py:336
Sparse Core Ops, SparseCore 0:
  32.8 69.0 all-gather.1

commit v3 on v2

v3 whole, which is shorter than its diff:
```python
import functools
import math

import jax
import jax.numpy as jnp
from jax import lax
from jax.experimental import pallas as pl
from jax.experimental.pallas import tpu as pltpu
from jax.sharding import PartitionSpec as P

TILE = 128
RING = 16
NEAR = 4
KEYS = 512
NEG = -1e30
NONE = -4000.0
FINE = 2.0**19
FULL = 32767.0


def plan_kernel(ring, per_row, slots, me_ref, sel_ref, place_ref, slot_ref, over_ref, count_ref):
    tiles, sel = sel_ref.shape
    capacity = place_ref.shape[0]
    rows = slot_ref.shape[0] // per_row
    me = me_ref[0]
    y, z = me // ring, lax.rem(me, ring)
    for i in range(capacity):
        place_ref[i] = 0
    for i in range(slot_ref.shape[0]):
        slot_ref[i] = -1

    def clear(i, _):
        count_ref[i] = 0
        return 0

    lax.fori_loop(0, count_ref.shape[0], clear, 0)

    def one_tile(t, carry):
        count, most = carry
        row, k = t // per_row, lax.rem(t, per_row)
        hit = jnp.int32(-1)
        for i in range(sel):
            b = sel_ref[t, i]
            slot = count_ref[b * rows + row]
            count_ref[b * rows + row] = slot + 1
            most = jnp.maximum(most, slot + 1)
            hit = jnp.where(b == me, slot, hit)

            @pl.when((row == y) & (lax.rem(b, ring) == z))
            def _():
                slot_ref[(b // ring) * per_row + k] = slot

        @pl.when(hit >= 0)
        def _():
            place_ref[jnp.minimum(count, capacity - 1)] = row * capacity + hit

        return count + jnp.where(hit >= 0, 1, 0), most

    _, most = lax.fori_loop(0, tiles, one_tile, (jnp.int32(0), jnp.int32(0)))
    over_ref[0] = jnp.where(most > slots, 1, 0)


def plan(selected, me, ring, per_row, slots, capacity, rows_of_chips):
    smem = pl.BlockSpec(memory_space=pltpu.SMEM)
    return pl.pallas_call(
        functools.partial(plan_kernel, ring, per_row, slots),
        out_shape=(
            jax.ShapeDtypeStruct((capacity,), jnp.int32),
            jax.ShapeDtypeStruct((rows_of_chips * per_row,), jnp.int32),
            jax.ShapeDtypeStruct((1,), jnp.int32),
        ),
        in_specs=[smem, smem],
        out_specs=(smem, smem, smem),
        scratch_shapes=[pltpu.SMEM((ring * rows_of_chips * rows_of_chips,), jnp.int32)],
        name="plan",
    )(me, selected)


def gather_kernel(slots, slot_ref, q_ref, kv_ref, first_ref, rest_ref, sem, kv_sem):
    near, sides, far, rows, _ = q_ref.shape
    columns = first_ref.shape[0]
    per_row = near * far
    tail = first_ref.shape[1] - kv_ref.shape[0]

    def tile(c, k, side, ref, slot):
        start = pl.multiple_of((slot * sides + side) * rows, rows)
        return pltpu.make_async_copy(
            q_ref.at[lax.rem(k, near), side, k // near],
            ref.at[c, pl.ds(start, rows)],
            sem.at[c * per_row + k, side],
        )

    def each(act):
        def one(i, _):
            c, k = i // per_row, lax.rem(i, per_row)
            slot = slot_ref[i]
            for side in range(sides):

                @pl.when((slot >= 0) & (slot < slots))
                def _():
                    act(tile(c, k, side, first_ref, slot))

                @pl.when(slot >= slots)
                def _():
                    act(tile(c, k, side, rest_ref, slot - slots))

            return 0

        lax.fori_loop(0, columns * per_row, one, 0)
        for c in range(columns):
            act(
                pltpu.make_async_copy(
                    kv_ref, first_ref.at[c, tail : tail + kv_ref.shape[0]], kv_sem.at[c]
                )
            )

    each(lambda copy: copy.start())
    each(lambda copy: copy.wait())


def gather_tiles(slots, capacity, slot, q, kv, columns):
    near, sides, far, rows, _ = q.shape
    full = sides * rows
    anywhere = pl.BlockSpec(memory_space=pl.ANY)
    return pl.pallas_call(
        functools.partial(gather_kernel, slots),
        out_shape=(
            jax.ShapeDtypeStruct((columns, slots * full + kv.shape[0], 128), q.dtype),
            jax.ShapeDtypeStruct((columns, (capacity - slots) * full, 128), q.dtype),
        ),
        in_specs=[pl.BlockSpec(memory_space=pltpu.SMEM), anywhere, anywhere],
        out_specs=(anywhere, anywhere),
        scratch_shapes=[
            pltpu.SemaphoreType.DMA((columns * near * far, sides)),
            pltpu.SemaphoreType.DMA((columns,)),
        ],
        name="gather_tiles",
    )(slot, q, kv)


def row_to_columns(row):
    return jnp.broadcast_to(row, (128, row.shape[1])).T


def pack(out_view, acc, level):
    rows = acc.shape[0]
    largest = jnp.maximum(jnp.max(jnp.abs(acc), axis=1, keepdims=True), 1e-30)
    code = jnp.round(acc * (FULL / largest)).astype(jnp.int32)
    out_view[0:rows, :] = code.astype(jnp.int16)
    lane = lax.broadcasted_iota(jnp.int32, (rows, 128), 1)
    both = jnp.where(lane == 0, level, jnp.log2(largest)).T[0:8, :]
    whole = jnp.round(jnp.clip(both, NONE, -NONE) * FINE).astype(jnp.int32)
    high = whole >> 16
    low = (whole & 0xFFFF) - 32768
    rank = lax.broadcasted_iota(jnp.int32, (8, 128), 0)
    stats = jnp.zeros((8, 128), jnp.int32)
    n = rows // 128
    for k, source in enumerate((high, low)):
        for stat in range(2):
            for g in range(n):
                piece = jnp.broadcast_to(source[stat : stat + 1, g * 128 : (g + 1) * 128], (8, 128))
                stats = jnp.where(rank == (k * 2 + stat) * n + g, piece, stats)
    out_view[rows : rows + 8, :] = stats.astype(jnp.int16)


def unpack_stats(view, rows):
    n = rows // 128
    raw = view[rows : rows + 8, :].astype(jnp.int32)
    found = []
    for stat in range(2):
        high = [raw[stat * n + g : stat * n + g + 1, :] for g in range(n)]
        low = [raw[(2 + stat) * n + g : (2 + stat) * n + g + 1, :] for g in range(n)]
        whole = [(h << 16) + (w + 32768) for h, w in zip(high, low)]
        found.append(jnp.concatenate([w.astype(jnp.float32) for w in whole], axis=1) * (1.0 / FINE))
    return found


def block_kernel(
    factor,
    slots,
    place_ref,
    valid_ref,
    q_ref,
    rest_ref,
    next_ref,
    next_rest_ref,
    kt_ref,
    v_ref,
    out_ref,
    out_rest_ref,
    s0_ref,
    s1_ref,
    top_ref,
    total_ref,
    acc_ref,
    held_ref,
    sem,
):
    i = pl.program_id(0)
    last = pl.num_programs(0) - 1
    length = kt_ref.shape[1]
    rows = q_ref.shape[1] // 2
    valid = valid_ref[0]
    steps = length // KEYS
    capacity = slots + out_rest_ref.shape[1]

    def score(q, s_ref, slot, j):
        s = jnp.dot(q, kt_ref[:, j * KEYS : (j + 1) * KEYS], preferred_element_type=jnp.float32)
        position = lax.broadcasted_iota(jnp.int32, (1, KEYS), 1) + j * KEYS
        s = s + jnp.where(position < valid, 0.0, NEG)
        s_ref[:, j * KEYS : (j + 1) * KEYS] = s
        best = s[:, 0:128]
        for g in range(1, KEYS // 128):
            best = jnp.maximum(best, s[:, g * 128 : (g + 1) * 128])
        if j:
            best = jnp.maximum(best, top_ref[slot])
        if j == steps - 1:
            best = jnp.broadcast_to(jnp.max(best, axis=1, keepdims=True), (rows, 128))
        top_ref[slot] = best

    def weigh(s_ref, slot, j):
        tops = jnp.concatenate([top_ref[slot]] * (KEYS // 128), axis=1)
        p = jnp.exp2((s_ref[:, j * KEYS : (j + 1) * KEYS] - tops) * factor)
        total = p[:, 0:128]
        for g in range(1, KEYS // 128):
            total += p[:, g * 128 : (g + 1) * 128]
        product = jnp.dot(
            p.astype(jnp.bfloat16), v_ref[j * KEYS : (j + 1) * KEYS, :], preferred_element_type=jnp.float32
        )
        total_ref[...] = total_ref[...] + total if j else total
        acc_ref[...] = acc_ref[...] + product if j else product

    def each_target(step, act):
        place = place_ref[step]
        row, slot = place // capacity, lax.rem(place, capacity)

        @pl.when(slot < slots)
        def _():
            act(pltpu.make_async_copy(held_ref, out_ref.at[row, slot], sem))

        @pl.when(slot >= slots)
        def _():
            act(pltpu.make_async_copy(held_ref, out_rest_ref.at[row, slot - slots], sem))

    def finish(side):
        total = jnp.sum(total_ref[...], axis=1, keepdims=True)
        level = top_ref[side][:, 0:1] * factor + jnp.log2(total)
        level = jnp.where(valid > 0, level, NONE)
        pack(held_ref.at[side], acc_ref[...] / total, level)

    def choose(step, ref, other, side):
        rest = lax.rem(place_ref[step], capacity) >= slots
        here = slice(side * rows, (side + 1) * rows)
        return jnp.where(rest, other[0, here, :], ref[0, here, :])

    @pl.when(i == 0)
    def _():
        q = choose(i, q_ref, rest_ref, 0)
        for j in range(steps):
            score(q, s0_ref, 0, j)

    q = choose(i, q_ref, rest_ref, 1)
    for j in range(steps):
        score(q, s1_ref, 1, j)
        weigh(s0_ref, 0, j)

    @pl.when(i > 0)
    def _():
        each_target(i - 1, lambda copy: copy.wait())

    finish(0)
    q = choose(jnp.minimum(i + 1, last), next_ref, next_rest_ref, 0)
    for j in range(steps):
        score(q, s0_ref, 0, j)
        weigh(s1_ref, 1, j)
    finish(1)
    each_target(i, lambda copy: copy.start())

    @pl.when(i == last)
    def _():
        each_target(i, lambda copy: copy.wait())


def block_part(factor, slots, sides, full, place, valid, q, rest, kt, v):
    columns = q.shape[0]
    capacity = place.shape[0]
    extra = capacity - slots
    rows = full // sides

    def tiles(ahead, first):
        def index(i, t, n):
            at = t[jnp.minimum(i + ahead, capacity - 1)]
            row, slot = at // capacity, lax.rem(at, capacity)
            slot = jnp.minimum(slot, slots - 1) if first else jnp.maximum(slot - slots, 0)
            return (row, slot, 0)

        return pl.BlockSpec((1, full, 128), index)

    anywhere = pl.BlockSpec(memory_space=pl.ANY)
    return pl.pallas_call(
        functools.partial(block_kernel, factor, slots),
        out_shape=(
            jax.ShapeDtypeStruct((columns, slots, sides, rows + 8, 128), jnp.int16),
            jax.ShapeDtypeStruct((columns, extra, sides, rows + 8, 128), jnp.int16),
        ),
        grid_spec=pltpu.PrefetchScalarGridSpec(
            num_scalar_prefetch=2,
            grid=(capacity,),
            in_specs=[
                tiles(0, True),
                tiles(0, False),
                tiles(1, True),
                tiles(1, False),
                pl.BlockSpec(kt.shape, lambda i, t, n: (0, 0)),
                pl.BlockSpec(v.shape, lambda i, t, n: (0, 0)),
            ],
            out_specs=(anywhere, anywhere),
            scratch_shapes=[
                pltpu.VMEM((rows, kt.shape[1]), jnp.float32),
                pltpu.VMEM((rows, kt.shape[1]), jnp.float32),
                pltpu.VMEM((2, rows, 128), jnp.float32),
                pltpu.VMEM((rows, 128), jnp.float32),
                pltpu.VMEM((rows, 128), jnp.float32),
                pltpu.VMEM((sides, rows + 8, 128), jnp.int16),
                pltpu.SemaphoreType.DMA,
            ],
        ),
        name="block_part",
    )(place, valid, q, rest, q, rest, kt, v)


def fresh_kernel(factor, ring, tokens, me_ref, q_ref, k_ref, v_ref, value_ref, level_ref):
    k = pl.program_id(0)
    y, z = me_ref[0], me_ref[1]
    _, sides, _, rows, _ = q_ref.shape
    keys = k_ref.shape[0]
    row = lax.broadcasted_iota(jnp.int32, (rows, 128), 0)
    lane = lax.broadcasted_iota(jnp.int32, (1, keys), 1)
    there = (lane // tokens * ring + z) * tokens + lax.rem(lane, tokens)
    for side in range(sides):
        s = lax.dot_general(
            q_ref[0, side, 0], k_ref[...], (((1,), (1,)), ((), ())), preferred_element_type=jnp.float32
        )
        here = (y * ring + k * sides + side) * tokens + lax.rem(row, tokens)
        allowed = there <= jnp.concatenate([here] * (keys // 128), axis=1)
        top = jnp.max(jnp.where(allowed, s, NEG), axis=1, keepdims=True)
        p = jnp.where(allowed, jnp.exp2((s - top) * factor), 0.0)
        high = p.astype(jnp.bfloat16)
        low = (p - high.astype(jnp.float32)).astype(jnp.bfloat16)
        acc = jnp.dot(high, v_ref[...], preferred_element_type=jnp.float32) + jnp.dot(
            low, v_ref[...], preferred_element_type=jnp.float32
        )
        total = jnp.maximum(jnp.sum(p, axis=1, keepdims=True), 1e-30)
        level = jnp.maximum(top * factor + jnp.log2(total), NONE)
        value_ref[0, side] = acc / total
        level_ref[0, side] = jnp.broadcast_to(level, (rows, 128))


def fresh_part(factor, ring, tokens, me, q, k, v):
    near, sides, far, rows, _ = q.shape
    per_row = near * far
    wide = jax.ShapeDtypeStruct((per_row, sides, rows, 128), jnp.float32)
    block = pl.BlockSpec((1, sides, rows, 128), lambda i, m: (i, 0, 0, 0))
    return pl.pallas_call(
        functools.partial(fresh_kernel, factor, ring, tokens),
        out_shape=(wide, wide),
        grid_spec=pltpu.PrefetchScalarGridSpec(
            num_scalar_prefetch=1,
            grid=(per_row,),
            in_specs=[
                pl.BlockSpec((1, sides, 1, rows, 128), lambda i, m: (lax.rem(i, near), 0, i // near, 0, 0)),
                pl.BlockSpec(k.shape, lambda i, m: (0, 0)),
                pl.BlockSpec(v.shape, lambda i, m: (0, 0)),
            ],
            out_specs=(block, block),
        ),
        name="fresh_part",
    )(me, q, k, v)


def column_kernel(slots, slot_ref, *refs):
    *part_refs, value_ref, level_ref, out_ref, acc_ref, top_ref, total_ref = refs
    k = pl.program_id(0)
    per_row = pl.num_programs(0)
    sources = len(part_refs) // 2
    _, sides, rows, _ = value_ref.shape
    for side in range(sides):
        acc_ref[side] = value_ref[0, side]
        top_ref[side] = level_ref[0, side]
        total_ref[side] = jnp.ones((rows, 128), jnp.float32)

    def add(ref):
        for side in range(sides):
            view = ref.at[0, 0, side]
            level, largest = unpack_stats(view, rows)
            level = row_to_columns(level)
            size = row_to_columns(jnp.exp2(largest) * (1.0 / FULL))
            old = top_ref[side]
            new = jnp.maximum(old, level)
            shrink = jnp.exp2(old - new)
            weight = jnp.exp2(level - new)
            value = view[0:rows, :].astype(jnp.int32).astype(jnp.float32)
            acc_ref[side] = acc_ref[side] * shrink + value * (weight * size)
            total_ref[side] = total_ref[side] * shrink + weight
            top_ref[side] = new

    for c in range(sources):
        slot = slot_ref[c * per_row + k]
        pl.when((slot >= 0) & (slot < slots))(functools.partial(add, part_refs[2 * c]))
        pl.when(slot >= slots)(functools.partial(add, part_refs[2 * c + 1]))

    for side in range(sides):
        total = total_ref[side]
        level = jnp.maximum(top_ref[side] + jnp.log2(total), NONE)[:, 0:1]
        pack(out_ref.at[0, side, 0], acc_ref[side] / total, level)


def column_part(slots, near, far, slot, got, rest, value, level):
    columns, _, sides, padded, _ = got.shape
    per_row = near * far
    rows = padded - 8

    def source(c, first):
        def index(i, t):
            at = t[c * per_row + i]
            return (c, jnp.clip(at, 0, slots - 1) if first else jnp.maximum(at - slots, 0), 0, 0, 0)

        return pl.BlockSpec((1, 1, sides, padded, 128), index)

    wide = pl.BlockSpec((1, sides, rows, 128), lambda i, t: (i, 0, 0, 0))
    return pl.pallas_call(
        functools.partial(column_kernel, slots),
        out_shape=jax.ShapeDtypeStruct((near, sides, far, padded, 128), jnp.int16),
        grid_spec=pltpu.PrefetchScalarGridSpec(
            num_scalar_prefetch=1,
            grid=(per_row,),
            in_specs=[source(c, first) for c in range(columns) for first in (True, False)] + [wide, wide],
            out_specs=pl.BlockSpec((1, sides, 1, padded, 128), lambda i, t: (lax.rem(i, near), 0, i // near, 0, 0)),
            scratch_shapes=[pltpu.VMEM((sides, rows, 128), jnp.float32)] * 3,
        ),
        name="column_part",
    )(slot, *[x for c in range(columns) for x in (got, rest)], value, level)


def joined(views, rows):
    stats = [unpack_stats(view, rows) for view in views]
    top = functools.reduce(jnp.maximum, [level for level, _ in stats])
    weights = [jnp.exp2(level - top) for level, _ in stats]
    total = functools.reduce(jnp.add, weights)
    acc = jnp.zeros((rows, 128), jnp.float32)
    for view, weight, (_, largest) in zip(views, weights, stats):
        share = row_to_columns(weight * jnp.exp2(largest) / (FULL * total))
        acc += view[0:rows, :].astype(jnp.int32).astype(jnp.float32) * share
    return acc, top + jnp.log2(total)


def near_kernel(got_ref, out_ref):
    sources, _, padded, _ = got_ref.shape
    acc, level = joined([got_ref.at[s, 0] for s in range(sources)], padded - 8)
    pack(out_ref.at[0], acc, row_to_columns(jnp.maximum(level, NONE))[:, 0:1])


def near_part(got):
    sources, places, padded, _ = got.shape
    return pl.pallas_call(
        near_kernel,
        out_shape=jax.ShapeDtypeStruct((places, padded, 128), jnp.int16),
        grid=(places,),
        in_specs=[pl.BlockSpec((sources, 1, padded, 128), lambda i: (0, i, 0, 0))],
        out_specs=pl.BlockSpec((1, padded, 128), lambda i: (i, 0, 0)),
        name="near_part",
    )(got)


def far_kernel(got_ref, out_ref):
    sources, padded, _ = got_ref.shape
    acc, _ = joined([got_ref.at[s] for s in range(sources)], padded - 8)
    out_ref[...] = acc.astype(jnp.bfloat16)


def far_part(got):
    vmem = pl.BlockSpec(memory_space=pltpu.VMEM)
    return pl.pallas_call(
        far_kernel,
        out_shape=jax.ShapeDtypeStruct((got.shape[1] - 8, 128), jnp.bfloat16),
        in_specs=[vmem],
        out_specs=vmem,
        name="far_part",
    )(got)


def shards(queries, fresh_keys, fresh_values, cache_keys, cache_values, selected, start):
    part, q_heads, head_size = queries.shape
    kv_heads = fresh_keys.shape[1]
    group = q_heads // kv_heads
    heads_axis = lax.axis_size("head")
    ctx_size = lax.axis_size("ctx")
    ctx_index = lax.axis_index("ctx")
    ring, near = RING, NEAR
    far = ring // near
    columns = ctx_size // ring
    across = [[y * ring + z for y in range(columns)] for z in range(ring)]
    close = [[y * ring + a * near + b for b in range(near)] for y in range(columns) for a in range(far)]
    wide = [[y * ring + a * near + b for a in range(far)] for y in range(columns) for b in range(near)]
    tokens = part * heads_axis
    sides = TILE // tokens
    per_row = ring // sides
    tiles, sel = selected.shape
    capacity = tiles * sel // ctx_size
    factor = head_size**-0.5 * math.log2(math.e)
    length = cache_keys.shape[0]

    mixed = jnp.concatenate(
        [
            queries.reshape(part, kv_heads, group, head_size),
            fresh_keys[:, :, None],
            fresh_values[:, :, None],
        ],
        axis=2,
    ).transpose(1, 2, 0, 3)
    mixed = lax.all_to_all(mixed, "head", split_axis=0, concat_axis=0, tiled=True)
    mixed = mixed.transpose(1, 0, 2, 3).reshape(group + 2, tokens, head_size)

    def exchange(x, groups):
        return lax.all_to_all(
            x, "ctx", split_axis=0, concat_axis=0, tiled=True, axis_index_groups=groups
        )

    def copies(x, n):
        return jnp.broadcast_to(x[None], (n,) + x.shape)

    me = jnp.stack([ctx_index // ring, ctx_index % ring])
    kt = cache_keys[:, 0].T
    v = cache_values[:, 0]
    slots = max(1, capacity - 1)
    place, slot, over = plan(selected, ctx_index.reshape(1), ring, per_row, slots, capacity, columns)
    valid = jnp.clip(start - ctx_index * length, 0, length)
    rows = group * tokens
    places = near // sides

    def rarely(x):
        return lax.cond(over[0] > 0, lambda a: exchange(a, across), lambda a: a, x)

    q = exchange(copies(mixed[:group].reshape(rows, head_size), far), wide)
    q = exchange(copies(q, near), close)
    q = q.reshape(places, sides, far, rows, head_size)
    first, rest = gather_tiles(
        slots, capacity, slot, q, mixed[group:].reshape(2 * tokens, head_size), columns
    )
    first, rest = lax.optimization_barrier((exchange(first, across), rest))
    rest = rarely(rest)
    column = first[:, -2 * tokens :].reshape(columns, 2, tokens, head_size)
    column_k = column[:, 0].reshape(columns * tokens, head_size)
    column_v = column[:, 1].reshape(columns * tokens, head_size)

    sent, sent_rest = block_part(factor, slots, sides, sides * rows, place, valid, first, rest, kt, v)
    got, sent_rest = lax.optimization_barrier((exchange(sent, across), sent_rest))
    got_rest = rarely(sent_rest)
    value, level = fresh_part(factor, ring, tokens, me, q, column_k, column_v)
    sent = column_part(slots, places, far, slot, got, got_rest, value, level)
    got = exchange(sent.reshape(near, far, rows + 8, head_size), close)
    got = exchange(near_part(got), wide)
    result = far_part(got)
    result = result.reshape(group, heads_axis, part, head_size).transpose(1, 0, 2, 3)
    result = lax.all_to_all(result, "head", split_axis=0, concat_axis=0, tiled=True)
    return result.reshape(q_heads, part, head_size).transpose(1, 0, 2)


def solution(mesh):
    in_specs = (
        P(("ctx", "head"), None, None),
        P(("ctx", "head"), None, None),
        P(("ctx", "head"), None, None),
        P("ctx", "head", None),
        P("ctx", "head", None),
        P(),
        P(),
    )
    out_specs = P(("ctx", "head"), None, None)
    return jax.shard_map(shards, mesh=mesh, in_specs=in_specs, out_specs=out_specs, check_vma=False)
```

time: 275 us -> 309 us (1.12)
  starting transfers between devices: 4.85 us -> 48.9 us
  waiting for transfers between devices: 100 us -> 65.7 us
  Pallas kernels: 48.4 us -> 76.5 us
  between operations: 14.1 us -> 1.39 us
  blocking collectives: 97.1 us -> 102 us
  local copies, waits for them, and re-layouts: 8.21 us -> 12.9 us
    all_gather x1 -> x0, waiting for transfers between devices: 60.4 us -> none  [shards(): lax.all_gather(column_q, 'ctx', axis=0, tiled=True, axis_index_groups=along)]
    all_to_all x1 -> x3, starting transfers between devices: 4.85 us -> 48.9 us  [exchange(): lax.all_to_all(x, 'ctx', split_axis=0, concat_axis=0, tiled=True, axis_in...]
    pallas_call x4 -> x7, Pallas kernels: 48.4 us -> 76.5 us  [the longest x1 23.7 us: block_part(): pl.pallas_call(functools.partial(block_kernel, factor, slots), out_shape=...]
    all_to_all x1 -> x3, waiting for transfers between devices: 39.6 us -> 65.7 us  [exchange(): lax.all_to_all(x, 'ctx', split_axis=0, concat_axis=0, tiled=True, axis_in...]
    all_to_all x2 -> x3, blocking collectives: 60.3 us -> 74.9 us  [exchange(): lax.all_to_all(x, 'ctx', split_axis=0, concat_axis=0, tiled=True, axis_in...]
    all_to_all x1, blocking collectives: 22.6 us -> 12.5 us  [shards(): lax.all_to_all(result, 'head', split_axis=0, concat_axis=0, tiled=True)]
    unnamed x3 -> x13, local copies, waits for them, and re-layouts: 4.51 us -> 8.1 us
  transfers between devices with their start and end apart: 2 -> 3, of which waited for: 2 -> 3; matrix products, arithmetic and copies ran while one was open for 2% -> 2% of each run, Pallas kernels for 2% -> 5%
where the time goes in v3:
time: 309 us; the launch traced here: 308 us
  blocking collectives  102 us (33%)
  Pallas kernels  76.5 us (25%)
  waiting for transfers between devices  65.7 us (21%)
  starting transfers between devices  48.9 us (16%)
  local copies, waits for them, and re-layouts  12.9 us (4%)
    all_to_all x3, blocking collectives, exchange(): lax.all_to_all(x, 'ctx', split_axis=0, concat_axis=0, tiled=True, axis_in...  74.9 us
    all_to_all x3, waiting for transfers between devices, exchange(): lax.all_to_all(x, 'ctx', split_axis=0, concat_axis=0, tiled=True, axis_in...  65.7 us
    all_to_all x3, starting transfers between devices, exchange(): lax.all_to_all(x, 'ctx', split_axis=0, concat_axis=0, tiled=True, axis_in...  48.9 us
    pallas_call x1, Pallas kernels, block_part(): pl.pallas_call(functools.partial(block_kernel, factor, slots), out_shape=...  23.7 us
    pallas_call x1, Pallas kernels, gather_tiles(): pl.pallas_call(functools.partial(gather_kernel, slots), out_shape=(jax.Sh...  22.4 us
    all_to_all x1, blocking collectives, shards(): lax.all_to_all(mixed, 'head', split_axis=0, concat_axis=0, tiled=True)  14.2 us
    all_to_all x1, blocking collectives, shards(): lax.all_to_all(result, 'head', split_axis=0, concat_axis=0, tiled=True)  12.5 us
    pallas_call x1, Pallas kernels, column_part(): pl.pallas_call(functools.partial(column_kernel, slots), out_shape=jax.Sha...  9.07 us
  transfers between devices with their start and end apart: 3, of which 3 were waited for; matrix products, arithmetic and copies ran while one was open for 2% of the time, Pallas kernels for 5%

profile of v3, /device:TPU:1, one launch (start us, length us, event | category | flops | bytes accessed | tf_op | source)
XLA Modules:
  0.0 307.6 jit_solution(1822673184382748446)
XLA Ops:
  0.0 0.0 copy-start.4
  0.0 0.9 copy.27
  0.9 0.7 copy_bitcast_fusion.3
  1.6 14.2 %all_to_all.50 = bf16[8,6,8,128]{3,2,1,0:T(8,128)(2,1)S(1)} all-to-all(bf16[8,6,8,128]{3,2,1,0:T(8,128)(2,1)S(1)} %maximum_bitcast_fusion), channel_id=1, replica_groups=mesh['ctx'=64,'head'=8] {'head'}, dimensions={0} | all-to-all | bytes 196608 | tf_op jit(solution)/shard_map/all_to_all | solution.py:521
  15.9 25.0 %all_to_all.51 = bf16[4,256,128]{2,1,0:T(8,128)(2,1)S(1)} all-to-all(bf16[4,256,128]{2,1,0:T(8,128)(2,1)S(1)} %broadcast_in_dim.22), channel_id=1, replica_groups={{0,32,64,96},{8,40,72,104},{16,48,80,112},{24,56,88,120},{128,160,192,2..., dimensions={0} | all-to-all | bytes 524288 | tf_op jit(solution)/shard_map/all_to_all | solution.py:525
  41.0 1.2 broadcast_in_dim.23
  42.2 9.3 %all-to-all-start.4 = ((bf16[4,4,256,128]{3,2,1,0:T(8,128)(2,1)}), bf16[4,4,256,128]{3,2,1,0:T(8,128)(2,1)S(1)}, u32[]{:S(2)}, u32[]{:S(2)}) async-start(bf16[4,4,256,128]{3,2,1,0:T(8,128)(2,1)} %broadcast_in_dim.23), calls=%async_computation.4 | async-start | bytes 2097152 | tf_op jit(solution)/shard_map/all_to_all | solution.py:525
  51.5 0.0 copy-done.4
  51.5 0.7 copy.26.sel_ref
  52.1 7.0 %plan.1 = (s32[6]{0:T(128)}, s32[32]{0:T(128)}, s32[1]{0:T(128)}) custom-call(s32[1]{0:T(128)} %bitcast.me_ref, s32[32,12]{1,0:T(8,128)} %copy.26.sel_ref), custom_call_target="tpu_custom_call" | custom-call | tf_op jit(solution)/shard_map/plan/pallas_call | solution.py:65
  59.2 0.6 slice.23
  59.8 16.9 %all-to-all-done.4 = bf16[4,4,256,128]{3,2,1,0:T(8,128)(2,1)S(1)} async-done(((bf16[4,4,256,128]{3,2,1,0:T(8,128)(2,1)}), bf16[4,4,256,128]{3,2,1,0:T(8,128)(2,1)S(1)}, u32[]{:S(2)}, u32[]{:S(2)}) %all-to-all-start.4) | async-done | bytes 1048608 | tf_op jit(solution)/shard_map/all_to_all | solution.py:525
  76.7 0.0 copy-start.2
  76.7 1.0 copy-done.2
  77.7 22.4 %gather_tiles.1 = (bf16[4,2688,128]{2,1,0:T(8,128)(2,1)}, bf16[4,512,128]{2,1,0:T(8,128)(2,1)S(1)}) custom-call(s32[32]{0:T(128)} %get-tuple-element.28.slot_ref, bf16[2,2,4,256,128]{4,3,2,1,0:T(8,128)(2,1)} %bitcast.39, bf16[128,128]{1,0:T(8,128)(2,1)} %bitcast.53), custom_call_target="tpu_custom_call" | custom-call | tf_op jit(solution)/shard_map/gather_tiles/pallas_call | solution.py:125
  100.1 35.8 %all-to-all-start.5 = ((bf16[4,2688,128]{2,1,0:T(8,128)(2,1)}), bf16[4,2688,128]{2,1,0:T(8,128)(2,1)S(1)}, u32[]{:S(2)}, u32[]{:S(2)}) async-start(bf16[4,2688,128]{2,1,0:T(8,128)(2,1)} %get-tuple-element.30), calls=%async_computation.5 | async-start | bytes 5505024 | tf_op jit(solution)/shard_map/all_to_all | solution.py:525
  137.2 2.3 copy.31
  139.5 28.2 %all-to-all-done.5.q_ref.next_ref = bf16[4,2688,128]{2,1,0:T(8,128)(2,1)S(1)} async-done(((bf16[4,2688,128]{2,1,0:T(8,128)(2,1)}), bf16[4,2688,128]{2,1,0:T(8,128)(2,1)S(1)}, u32[]{:S(2)}, u32[]{:S(2)}) %all-to-all-start.5) | async-done | bytes 2752544 | tf_op jit(solution)/shard_map/all_to_all | solution.py:525
  167.7 0.0 copy-start.1
  167.7 0.0 copy-start.3
  167.7 0.9 copy-done.3
  168.6 0.9 copy-done.1
  169.5 23.7 %block_part.1 = (s16[4,5,2,264,128]{4,3,2,1,0:T(8,128)(2,1)}, s16[4,1,2,264,128]{4,3,2,1,0:T(8,128)(2,1)S(1)}) custom-call(s32[6]{0:T(128)} %get-tuple-element.29.place_ref, s32[1]{0:T(128)S(6)} %min.6.valid_ref, bf16[4,2688,128]{2,1,0:T(8,128)(2,1)} %copy-done.1, bf16[4,512,128]{2,1,0:T(8,128)(2,1)} %copy-done.3, bf16[4,2688,128]{2,1,0:T(8,128)(2,1)} %copy-done.1, ...), custom_call_target="tpu_custom_call" | custom-call | tf_op jit(solution)/shard_map/block_part/pallas_call | solution.py:300
  193.2 0.0 slice-start
  193.2 3.8 %all-to-all-start.6 = ((s16[4,5,2,264,128]{4,3,2,1,0:T(8,128)(2,1)}), s16[4,5,2,264,128]{4,3,2,1,0:T(8,128)(2,1)S(1)}, u32[]{:S(2)}, u32[]{:S(2)}) async-start(s16[4,5,2,264,128]{4,3,2,1,0:T(8,128)(2,1)} %get-tuple-element.35), calls=%async_computation.6 | async-start | bytes 5406720 | tf_op jit(solution)/shard_map/all_to_all | solution.py:525
  197.0 0.6 pad_add_fusion.me_ref
  197.6 0.0 slice-done
  197.6 0.7 fusion
  198.3 8.5 %fresh_part.1 = (f32[8,2,256,128]{3,2,1,0:T(8,128)}, f32[8,2,256,128]{3,2,1,0:T(8,128)}) custom-call(s32[2]{0:T(128)} %pad_add_fusion.me_ref, bf16[2,2,4,256,128]{4,3,2,1,0:T(8,128)(2,1)} %bitcast.40, bf16[256,128]{1,0:T(8,128)(2,1)} %bitcast.49, bf16[256,128]{1,0:T(8,128)(2,1)} %bitcast.48), custom_call_target="tpu_custom_call" | custom-call | tf_op jit(solution)/shard_map/fresh_part/pallas_call | solution.py:364
  206.8 20.5 %all-to-all-done.6.refs_0_.refs_2_.refs_4_.refs_6_ = s16[4,5,2,264,128]{4,3,2,1,0:T(8,128)(2,1)S(1)} async-done(((s16[4,5,2,264,128]{4,3,2,1,0:T(8,128)(2,1)}), s16[4,5,2,264,128]{4,3,2,1,0:T(8,128)(2,1)S(1)}, u32[]{:S(2)}, u32[]{:S(2)}) %all-to-all-start.6) | async-done | bytes 2703392 | tf_op jit(solution)/shard_map/all_to_all | solution.py:525
  227.3 0.0 copy-start
  227.3 1.5 copy-done
  228.9 9.1 %column_part.1 = s16[2,2,4,264,128]{4,3,2,1,0:T(8,128)(2,1)} custom-call(s32[32]{0:T(128)} %get-tuple-element.28.slot_ref, s16[4,5,2,264,128]{4,3,2,1,0:T(8,128)(2,1)} %copy-done, s16[4,1,2,264,128]{4,3,2,1,0:T(8,128)(2,1)S(1)} %get-tuple-element.46.refs_1_.refs_3_.refs_5_.refs_7_, s16[4,5,2,264,128]{4,3,2,1,0:T(8,128)(2,1)} %copy-done, ...), custom_call_target="tpu_custom_call" | custom-call | tf_op jit(solution)/shard_map/column_part/pallas_call | solution.py:431
  237.9 29.0 %all_to_all.52.got_ref = s16[4,4,264,128]{3,2,1,0:T(8,128)(2,1)} all-to-all(s16[4,4,264,128]{3,2,1,0:T(8,128)(2,1)} %bitcast.41), channel_id=1, replica_groups={{0,8,16,24},{32,40,48,56},{64,72,80,88},{96,104,112,120},{128,136,144,1..., dimensions={0} | all-to-all | bytes 2162688 | tf_op jit(solution)/shard_map/all_to_all | solution.py:525
  267.0 4.1 %near_part.1 = s16[4,264,128]{2,1,0:T(8,128)(2,1)} custom-call(s16[4,4,264,128]{3,2,1,0:T(8,128)(2,1)} %all_to_all.52.got_ref), custom_call_target="tpu_custom_call" | custom-call | tf_op jit(solution)/shard_map/near_part/pallas_call | solution.py:465
  271.0 20.8 %all_to_all.53.got_ref = s16[4,264,128]{2,1,0:T(8,128)(2,1)} all-to-all(s16[4,264,128]{2,1,0:T(8,128)(2,1)} %near_part.1), channel_id=1, replica_groups={{0,32,64,96},{8,40,72,104},{16,48,80,112},{24,56,88,120},{128,160,192,2..., dimensions={0} | all-to-all | bytes 540672 | tf_op jit(solution)/shard_map/all_to_all | solution.py:525
  291.8 1.8 far_part.1
  293.7 0.9 copy.45
  294.5 12.5 %all_to_all.54 = bf16[8,4,8,128]{3,2,1,0:T(8,128)(2,1)S(1)} all-to-all(bf16[8,4,8,128]{3,2,1,0:T(8,128)(2,1)S(1)} %bitcast.50), channel_id=1, replica_groups=mesh['ctx'=64,'head'=8] {'head'}, dimensions={0} | all-to-all | bytes 131072 | tf_op jit(solution)/shard_map/all_to_all | solution.py:565
  307.0 0.6 copy.44
  (6 shorter events, 0.1 us)
Async XLA Ops:
  0.0 51.5 %copy-start.4 = (s32[32,12]{0,1:T(8,128)S(1)}, s32[32,12]{0,1:T(8,128)}, u32[]{:S(2)}) copy-start(s32[32,12]{0,1:T(8,128)} %param.16) | copy-start | bytes 4612
  42.2 34.6 %all-to-all-start.4 = ((bf16[4,4,256,128]{3,2,1,0:T(8,128)(2,1)}), bf16[4,4,256,128]{3,2,1,0:T(8,128)(2,1)S(1)}, u32[]{:S(2)}, u32[]{:S(2)}) async-start(bf16[4,4,256,128]{3,2,1,0:T(8,128)(2,1)} %broadcast_in_dim.23), calls=%async_computation.4 | async-start | bytes 2097152 | tf_op jit(solution)/shard_map/all_to_all | solution.py:525
  76.7 1.0 copy-start.2
  100.1 67.6 %all-to-all-start.5 = ((bf16[4,2688,128]{2,1,0:T(8,128)(2,1)}), bf16[4,2688,128]{2,1,0:T(8,128)(2,1)S(1)}, u32[]{:S(2)}, u32[]{:S(2)}) async-start(bf16[4,2688,128]{2,1,0:T(8,128)(2,1)} %get-tuple-element.30), calls=%async_computation.5 | async-start | bytes 5505024 | tf_op jit(solution)/shard_map/all_to_all | solution.py:525
  167.7 1.7 copy-start.1
  167.7 0.9 copy-start.3
  193.2 4.5 %slice-start = ((bf16[4,2688,128]{2,1,0:T(8,128)(2,1)}), bf16[4,128,128]{2,1,0:T(8,128)(2,1)S(1)}, s32[]{:S(2)}) async-start(bf16[4,2688,128]{2,1,0:T(8,128)(2,1)} %copy-done.1), calls=%async_computation.10 | async-start | bytes 262144 | tf_op jit(solution)/shard_map/slice | solution.py:552
  193.2 34.2 %all-to-all-start.6 = ((s16[4,5,2,264,128]{4,3,2,1,0:T(8,128)(2,1)}), s16[4,5,2,264,128]{4,3,2,1,0:T(8,128)(2,1)S(1)}, u32[]{:S(2)}, u32[]{:S(2)}) async-start(s16[4,5,2,264,128]{4,3,2,1,0:T(8,128)(2,1)} %get-tuple-element.35), calls=%async_computation.6 | async-start | bytes 5406720 | tf_op jit(solution)/shard_map/all_to_all | solution.py:525
  227.3 1.5 copy-start

commit v4 on v3

v4 whole, which is shorter than its diff:
```python
import functools
import math

import jax
import jax.numpy as jnp
from jax import lax
from jax.experimental import pallas as pl
from jax.experimental.pallas import tpu as pltpu
from jax.sharding import PartitionSpec as P

TILE = 128
RING = 16
KEYS = 512
NEG = -1e30
NONE = -4000.0
FINE = 2.0**19
FULL = 32767.0


def plan_kernel(ring, per_row, cut, me_ref, sel_ref, place_ref, slot_ref, split_ref, over_ref, count_ref):
    tiles, sel = sel_ref.shape
    capacity = place_ref.shape[0]
    rows = slot_ref.shape[0] // per_row
    me = me_ref[0]
    y, z = me // ring, lax.rem(me, ring)
    for i in range(capacity):
        place_ref[i] = 0
    for i in range(slot_ref.shape[0]):
        slot_ref[i] = -1

    def clear(i, _):
        count_ref[i] = 0
        return 0

    lax.fori_loop(0, count_ref.shape[0], clear, 0)

    def one_tile(t, carry):
        front, back, most = carry
        row, k = t // per_row, lax.rem(t, per_row)
        hit = jnp.int32(-1)
        for i in range(sel):
            b = sel_ref[t, i]
            slot = count_ref[b * rows + row]
            count_ref[b * rows + row] = slot + 1
            most = jnp.maximum(most, slot + 1)
            hit = jnp.where(b == me, slot, hit)

            @pl.when((row == y) & (lax.rem(b, ring) == z))
            def _():
                slot_ref[(b // ring) * per_row + k] = slot

        early = (hit >= 0) & (hit < cut)

        @pl.when(hit >= 0)
        def _():
            at = jnp.where(early, jnp.minimum(front, capacity - 1), jnp.maximum(back, 0))
            place_ref[at] = row * capacity + hit

        front = front + jnp.where(early, 1, 0)
        back = back - jnp.where(hit >= cut, 1, 0)
        return front, back, most

    start = (jnp.int32(0), jnp.int32(capacity - 1), jnp.int32(0))
    front, _, most = lax.fori_loop(0, tiles, one_tile, start)
    split_ref[0] = jnp.minimum(front, capacity)
    over_ref[0] = jnp.where(most > capacity - 1, 1, 0)


def plan(selected, me, ring, per_row, cut, capacity, rows_of_chips):
    smem = pl.BlockSpec(memory_space=pltpu.SMEM)
    return pl.pallas_call(
        functools.partial(plan_kernel, ring, per_row, cut),
        out_shape=(
            jax.ShapeDtypeStruct((capacity,), jnp.int32),
            jax.ShapeDtypeStruct((rows_of_chips * per_row,), jnp.int32),
            jax.ShapeDtypeStruct((1,), jnp.int32),
            jax.ShapeDtypeStruct((1,), jnp.int32),
        ),
        in_specs=[smem, smem],
        out_specs=(smem, smem, smem, smem),
        scratch_shapes=[pltpu.SMEM((ring * rows_of_chips * rows_of_chips,), jnp.int32)],
        name="plan",
    )(me, selected)


def gather_kernel(groups, slot_ref, q_ref, kv_ref, *refs):
    *out_refs, sem, kv_sem = refs
    per_row, full, _ = q_ref.shape
    columns = out_refs[0].shape[0]
    behind = groups[0][1] * full

    def each(act):
        def one(i, _):
            c, k = i // per_row, lax.rem(i, per_row)
            slot = slot_ref[i]
            for (low, high), ref in zip(groups, out_refs):

                @pl.when((slot >= low) & (slot < high))
                def _():
                    start = pl.multiple_of((slot - low) * full, full)
                    act(pltpu.make_async_copy(q_ref.at[k], ref.at[c, pl.ds(start, full)], sem.at[i]))

            return 0

        lax.fori_loop(0, columns * per_row, one, 0)
        for c in range(columns):
            target = out_refs[0].at[c, behind : behind + kv_ref.shape[0]]
            act(pltpu.make_async_copy(kv_ref, target, kv_sem.at[c]))

    each(lambda copy: copy.start())
    each(lambda copy: copy.wait())


def gather_tiles(groups, slot, q, kv, columns):
    per_row, full, _ = q.shape
    anywhere = pl.BlockSpec(memory_space=pl.ANY)
    vmem = pl.BlockSpec(memory_space=pltpu.VMEM)
    heights = [(high - low) * full for low, high in groups]
    heights[0] += kv.shape[0]
    return pl.pallas_call(
        functools.partial(gather_kernel, groups),
        out_shape=[jax.ShapeDtypeStruct((columns, height, 128), q.dtype) for height in heights],
        in_specs=[pl.BlockSpec(memory_space=pltpu.SMEM), vmem, vmem],
        out_specs=[anywhere] * len(groups),
        scratch_shapes=[
            pltpu.SemaphoreType.DMA((columns * per_row,)),
            pltpu.SemaphoreType.DMA((columns,)),
        ],
        name="gather_tiles",
    )(slot, q, kv)


def row_to_columns(row):
    return jnp.broadcast_to(row, (128, row.shape[1])).T


def pack(out_view, acc, level):
    rows = acc.shape[0]
    largest = jnp.maximum(jnp.max(jnp.abs(acc), axis=1, keepdims=True), 1e-30)
    code = jnp.round(acc * (FULL / largest)).astype(jnp.int32)
    out_view[0:rows, :] = code.astype(jnp.int16)
    lane = lax.broadcasted_iota(jnp.int32, (rows, 128), 1)
    both = jnp.where(lane == 0, level, jnp.log2(largest)).T[0:8, :]
    whole = jnp.round(jnp.clip(both, NONE, -NONE) * FINE).astype(jnp.int32)
    high = whole >> 16
    low = (whole & 0xFFFF) - 32768
    rank = lax.broadcasted_iota(jnp.int32, (8, 128), 0)
    stats = jnp.zeros((8, 128), jnp.int32)
    n = rows // 128
    for k, source in enumerate((high, low)):
        for stat in range(2):
            for g in range(n):
                piece = jnp.broadcast_to(source[stat : stat + 1, g * 128 : (g + 1) * 128], (8, 128))
                stats = jnp.where(rank == (k * 2 + stat) * n + g, piece, stats)
    out_view[rows : rows + 8, :] = stats.astype(jnp.int16)


def unpack_stats(view, rows):
    n = rows // 128
    raw = view[rows : rows + 8, :].astype(jnp.int32)
    found = []
    for stat in range(2):
        high = [raw[stat * n + g : stat * n + g + 1, :] for g in range(n)]
        low = [raw[(2 + stat) * n + g : (2 + stat) * n + g + 1, :] for g in range(n)]
        whole = [(h << 16) + (w + 32768) for h, w in zip(high, low)]
        found.append(jnp.concatenate([w.astype(jnp.float32) for w in whole], axis=1) * (1.0 / FINE))
    return found


def block_kernel(factor, groups, capacity, place_ref, span_ref, valid_ref, *refs):
    n = len(groups)
    now_refs, next_refs = refs[0:n], refs[n : 2 * n]
    kt_ref, v_ref = refs[2 * n : 2 * n + 2]
    out_refs = refs[2 * n + 2 : 3 * n + 2]
    s0_ref, s1_ref, top_ref, total_ref, acc_ref, held_ref, sem = refs[3 * n + 2 :]
    i = pl.program_id(0)
    last = span_ref[1] - span_ref[0] - 1
    length = kt_ref.shape[1]
    rows = now_refs[0].shape[1] // 2
    valid = valid_ref[0]
    steps = length // KEYS

    def score(q, s_ref, slot, j):
        s = jnp.dot(q, kt_ref[:, j * KEYS : (j + 1) * KEYS], preferred_element_type=jnp.float32)
        position = lax.broadcasted_iota(jnp.int32, (1, KEYS), 1) + j * KEYS
        s = s + jnp.where(position < valid, 0.0, NEG)
        s_ref[:, j * KEYS : (j + 1) * KEYS] = s
        best = s[:, 0:128]
        for g in range(1, KEYS // 128):
            best = jnp.maximum(best, s[:, g * 128 : (g + 1) * 128])
        if j:
            best = jnp.maximum(best, top_ref[slot])
        if j == steps - 1:
            best = jnp.broadcast_to(jnp.max(best, axis=1, keepdims=True), (rows, 128))
        top_ref[slot] = best

    def weigh(s_ref, slot, j):
        tops = jnp.concatenate([top_ref[slot]] * (KEYS // 128), axis=1)
        p = jnp.exp2((s_ref[:, j * KEYS : (j + 1) * KEYS] - tops) * factor)
        total = p[:, 0:128]
        for g in range(1, KEYS // 128):
            total += p[:, g * 128 : (g + 1) * 128]
        product = jnp.dot(
            p.astype(jnp.bfloat16), v_ref[j * KEYS : (j + 1) * KEYS, :], preferred_element_type=jnp.float32
        )
        total_ref[...] = total_ref[...] + total if j else total
        acc_ref[...] = acc_ref[...] + product if j else product

    def place(step):
        return place_ref[jnp.clip(span_ref[0] + step, 0, capacity - 1)]

    def each_target(step, act):
        row, slot = place(step) // capacity, lax.rem(place(step), capacity)
        for (low, high), ref in zip(groups, out_refs):

            @pl.when((slot >= low) & (slot < high))
            def _():
                act(pltpu.make_async_copy(held_ref, ref.at[row, slot - low], sem))

    def finish(side):
        total = jnp.sum(total_ref[...], axis=1, keepdims=True)
        level = top_ref[side][:, 0:1] * factor + jnp.log2(total)
        level = jnp.where(valid > 0, level, NONE)
        pack(held_ref.at[side], acc_ref[...] / total, level)

    def choose(step, sources, side):
        slot = lax.rem(place(step), capacity)
        here = slice(side * rows, (side + 1) * rows)
        q = sources[0][0, here, :]
        for (low, _), ref in zip(groups[1:], sources[1:]):
            q = jnp.where(slot >= low, ref[0, here, :], q)
        return q

    @pl.when((i == 0) & (i <= last))
    def _():
        q = choose(i, now_refs, 0)
        for j in range(steps):
            score(q, s0_ref, 0, j)

    @pl.when(i <= last)
    def _():
        q = choose(i, now_refs, 1)
        for j in range(steps):
            score(q, s1_ref, 1, j)
            weigh(s0_ref, 0, j)

        @pl.when(i > 0)
        def _():
            each_target(i - 1, lambda copy: copy.wait())

        finish(0)
        q = choose(jnp.minimum(i + 1, last), next_refs, 0)
        for j in range(steps):
            score(q, s0_ref, 0, j)
            weigh(s1_ref, 1, j)
        finish(1)
        each_target(i, lambda copy: copy.start())

    @pl.when(i == last)
    def _():
        each_target(i, lambda copy: copy.wait())


def block_part(factor, groups, sides, full, place, span, valid, sources, kt, v):
    columns = sources[0].shape[0]
    capacity = place.shape[0]
    rows = full // sides

    def tiles(ahead, low, high):
        def index(i, t, s, n):
            at = t[jnp.clip(jnp.minimum(s[0] + i + ahead, s[1] - 1), 0, capacity - 1)]
            return (at // capacity, jnp.clip(lax.rem(at, capacity) - low, 0, high - low - 1), 0)

        return pl.BlockSpec((1, full, 128), index)

    whole = lambda i, t, s, n: (0, 0)
    anywhere = pl.BlockSpec(memory_space=pl.ANY)
    return pl.pallas_call(
        functools.partial(block_kernel, factor, groups, capacity),
        out_shape=[
            jax.ShapeDtypeStruct((columns, high - low, sides, rows + 8, 128), jnp.int16)
            for low, high in groups
        ],
        grid_spec=pltpu.PrefetchScalarGridSpec(
            num_scalar_prefetch=3,
            grid=(capacity,),
            in_specs=[tiles(0, *group) for group in groups]
            + [tiles(1, *group) for group in groups]
            + [pl.BlockSpec(kt.shape, whole), pl.BlockSpec(v.shape, whole)],
            out_specs=[anywhere] * len(groups),
            scratch_shapes=[
                pltpu.VMEM((rows, kt.shape[1]), jnp.float32),
                pltpu.VMEM((rows, kt.shape[1]), jnp.float32),
                pltpu.VMEM((2, rows, 128), jnp.float32),
                pltpu.VMEM((rows, 128), jnp.float32),
                pltpu.VMEM((rows, 128), jnp.float32),
                pltpu.VMEM((sides, rows + 8, 128), jnp.int16),
                pltpu.SemaphoreType.DMA,
            ],
        ),
        name="block_part",
    )(place, span, valid, *sources, *sources, kt, v)


def fresh_kernel(factor, ring, tokens, me_ref, q_ref, k_ref, v_ref, value_ref, level_ref):
    k = pl.program_id(0)
    y, z = me_ref[0], me_ref[1]
    _, sides, rows, _ = q_ref.shape
    keys = k_ref.shape[0]
    row = lax.broadcasted_iota(jnp.int32, (rows, 128), 0)
    lane = lax.broadcasted_iota(jnp.int32, (1, keys), 1)
    there = (lane // tokens * ring + z) * tokens + lax.rem(lane, tokens)
    for side in range(sides):
        s = lax.dot_general(
            q_ref[0, side], k_ref[...], (((1,), (1,)), ((), ())), preferred_element_type=jnp.float32
        )
        here = (y * ring + k * sides + side) * tokens + lax.rem(row, tokens)
        allowed = there <= jnp.concatenate([here] * (keys // 128), axis=1)
        top = jnp.max(jnp.where(allowed, s, NEG), axis=1, keepdims=True)
        p = jnp.where(allowed, jnp.exp2((s - top) * factor), 0.0)
        high = p.astype(jnp.bfloat16)
        low = (p - high.astype(jnp.float32)).astype(jnp.bfloat16)
        acc = jnp.dot(high, v_ref[...], preferred_element_type=jnp.float32) + jnp.dot(
            low, v_ref[...], preferred_element_type=jnp.float32
        )
        total = jnp.maximum(jnp.sum(p, axis=1, keepdims=True), 1e-30)
        level = jnp.maximum(top * factor + jnp.log2(total), NONE)
        value_ref[0, side] = acc / total
        level_ref[0, side] = jnp.broadcast_to(level, (rows, 128))


def fresh_part(factor, ring, tokens, me, q, k, v):
    per_row, sides, rows, _ = q.shape
    wide = jax.ShapeDtypeStruct((per_row, sides, rows, 128), jnp.float32)
    block = pl.BlockSpec((1, sides, rows, 128), lambda i, m: (i, 0, 0, 0))
    return pl.pallas_call(
        functools.partial(fresh_kernel, factor, ring, tokens),
        out_shape=(wide, wide),
        grid_spec=pltpu.PrefetchScalarGridSpec(
            num_scalar_prefetch=1,
            grid=(per_row,),
            in_specs=[
                block,
                pl.BlockSpec(k.shape, lambda i, m: (0, 0)),
                pl.BlockSpec(v.shape, lambda i, m: (0, 0)),
            ],
            out_specs=(block, block),
        ),
        name="fresh_part",
    )(me, q, k, v)


def column_kernel(groups, slot_ref, *refs):
    *part_refs, value_ref, level_ref, out_ref, acc_ref, top_ref, total_ref = refs
    k = pl.program_id(0)
    per_row = pl.num_programs(0)
    n = len(groups)
    sources = len(part_refs) // n
    _, sides, rows, _ = value_ref.shape
    for side in range(sides):
        acc_ref[side] = value_ref[0, side]
        top_ref[side] = level_ref[0, side]
        total_ref[side] = jnp.ones((rows, 128), jnp.float32)

    def add(ref):
        for side in range(sides):
            view = ref.at[0, 0, side]
            level, largest = unpack_stats(view, rows)
            level = row_to_columns(level)
            size = row_to_columns(jnp.exp2(largest) * (1.0 / FULL))
            old = top_ref[side]
            new = jnp.maximum(old, level)
            shrink = jnp.exp2(old - new)
            weight = jnp.exp2(level - new)
            value = view[0:rows, :].astype(jnp.int32).astype(jnp.float32)
            acc_ref[side] = acc_ref[side] * shrink + value * (weight * size)
            total_ref[side] = total_ref[side] * shrink + weight
            top_ref[side] = new

    for c in range(sources):
        slot = slot_ref[c * per_row + k]
        for g, (low, high) in enumerate(groups):
            pl.when((slot >= low) & (slot < high))(functools.partial(add, part_refs[n * c + g]))

    for side in range(sides):
        total = total_ref[side]
        level = jnp.maximum(top_ref[side] + jnp.log2(total), NONE)[:, 0:1]
        pack(out_ref.at[side], acc_ref[side] / total, level)


def column_part(groups, slot, got, value, level):
    columns, _, sides, padded, _ = got[0].shape
    per_row = value.shape[0]
    rows = padded - 8

    def source(c, low, high):
        def index(i, t):
            return (c, jnp.clip(t[c * per_row + i] - low, 0, high - low - 1), 0, 0, 0)

        return pl.BlockSpec((1, 1, sides, padded, 128), index)

    wide = pl.BlockSpec((1, sides, rows, 128), lambda i, t: (i, 0, 0, 0))
    return pl.pallas_call(
        functools.partial(column_kernel, groups),
        out_shape=jax.ShapeDtypeStruct((per_row * sides, padded, 128), jnp.int16),
        grid_spec=pltpu.PrefetchScalarGridSpec(
            num_scalar_prefetch=1,
            grid=(per_row,),
            in_specs=[source(c, *group) for c in range(columns) for group in groups] + [wide, wide],
            out_specs=pl.BlockSpec((sides, padded, 128), lambda i, t: (i, 0, 0)),
            scratch_shapes=[pltpu.VMEM((sides, rows, 128), jnp.float32)] * 3,
        ),
        name="column_part",
    )(slot, *[x for c in range(columns) for x in got], value, level)


def ring_kernel(got_ref, out_ref):
    sources, padded, _ = got_ref.shape
    rows = padded - 8
    stats = [unpack_stats(got_ref.at[s], rows) for s in range(sources)]
    top = functools.reduce(jnp.maximum, [level for level, _ in stats])
    weights = [jnp.exp2(level - top) for level, _ in stats]
    total = functools.reduce(jnp.add, weights)
    acc = jnp.zeros((rows, 128), jnp.float32)
    for s in range(sources):
        share = row_to_columns(weights[s] * jnp.exp2(stats[s][1]) / (FULL * total))
        acc += got_ref[s, 0:rows, :].astype(jnp.int32).astype(jnp.float32) * share
    out_ref[...] = acc.astype(jnp.bfloat16)


def ring_part(got):
    vmem = pl.BlockSpec(memory_space=pltpu.VMEM)
    return pl.pallas_call(
        ring_kernel,
        out_shape=jax.ShapeDtypeStruct((got.shape[1] - 8, 128), jnp.bfloat16),
        in_specs=[vmem],
        out_specs=vmem,
        name="ring_part",
    )(got)


def shards(queries, fresh_keys, fresh_values, cache_keys, cache_values, selected, start):
    part, q_heads, head_size = queries.shape
    kv_heads = fresh_keys.shape[1]
    group = q_heads // kv_heads
    heads_axis = lax.axis_size("head")
    ctx_size = lax.axis_size("ctx")
    ctx_index = lax.axis_index("ctx")
    ring = RING
    columns = ctx_size // ring
    across = [[y * ring + z for y in range(columns)] for z in range(ring)]
    along = [[y * ring + z for z in range(ring)] for y in range(columns)]
    tokens = part * heads_axis
    sides = TILE // tokens
    per_row = ring // sides
    tiles, sel = selected.shape
    capacity = tiles * sel // ctx_size
    factor = head_size**-0.5 * math.log2(math.e)
    length = cache_keys.shape[0]

    mixed = jnp.concatenate(
        [
            queries.reshape(part, kv_heads, group, head_size),
            fresh_keys[:, :, None],
            fresh_values[:, :, None],
        ],
        axis=2,
    ).transpose(1, 2, 0, 3)
    mixed = lax.all_to_all(mixed, "head", split_axis=0, concat_axis=0, tiled=True)
    mixed = mixed.transpose(1, 0, 2, 3).reshape(group + 2, tokens, head_size)

    def exchange(x, groups):
        return lax.all_to_all(
            x, "ctx", split_axis=0, concat_axis=0, tiled=True, axis_index_groups=groups
        )

    def copies(x, n):
        return jnp.broadcast_to(x[None], (n,) + x.shape)

    me = jnp.stack([ctx_index // ring, ctx_index % ring])
    kt = cache_keys[:, 0].T
    v = cache_values[:, 0]
    cut = max(1, (capacity - 1) // 2)
    early, late = [(0, cut)], [(cut, capacity - 1), (capacity - 1, capacity)]
    groups = early + late
    place, slot, split, over = plan(selected, ctx_index.reshape(1), ring, per_row, cut, capacity, columns)
    valid = jnp.clip(start - ctx_index * length, 0, length)
    rows = group * tokens
    full = sides * rows

    def send(x, after, seldom=False):
        if after is not None:
            x, after = lax.optimization_barrier((x, after))
        if seldom:
            return lax.cond(over[0] > 0, lambda a: exchange(a, across), lambda a: a, x), after
        return exchange(x, across), after

    q = exchange(copies(mixed[:group].reshape(rows, head_size), ring), along)
    q = q.reshape(per_row, full, head_size)
    first, second, third = gather_tiles(
        groups, slot, q, mixed[group:].reshape(2 * tokens, head_size), columns
    )
    first, _ = send(first, None)
    second, first = send(second, first)
    third, second = send(third, second, True)
    column = first[:, cut * full :].reshape(columns, 2, tokens, head_size)
    column_k = column[:, 0].reshape(columns * tokens, head_size)
    column_v = column[:, 1].reshape(columns * tokens, head_size)

    zero, end = jnp.zeros((1,), jnp.int32), jnp.full((1,), capacity, jnp.int32)
    first_span, late_span = jnp.concatenate([zero, split]), jnp.concatenate([split, end])
    (sent,) = block_part(factor, early, sides, full, place, first_span, valid, [first], kt, v)
    sent, late_span = lax.optimization_barrier((sent, late_span))
    sent_more, sent_rest = block_part(
        factor, late, sides, full, place, late_span, valid, [second, third], kt, v
    )
    got, _ = send(sent, None)
    got_more, got = send(sent_more, got)
    got_rest, got_more = send(sent_rest, got_more, True)
    value, level = fresh_part(
        factor, ring, tokens, me, q.reshape(per_row, sides, rows, head_size), column_k, column_v
    )
    sent = column_part(groups, slot, [got, got_more, got_rest], value, level)
    result = ring_part(exchange(sent, along))
    result = result.reshape(group, heads_axis, part, head_size).transpose(1, 0, 2, 3)
    result = lax.all_to_all(result, "head", split_axis=0, concat_axis=0, tiled=True)
    return result.reshape(q_heads, part, head_size).transpose(1, 0, 2)


def solution(mesh):
    in_specs = (
        P(("ctx", "head"), None, None),
        P(("ctx", "head"), None, None),
        P(("ctx", "head"), None, None),
        P("ctx", "head", None),
        P("ctx", "head", None),
        P(),
        P(),
    )
    out_specs = P(("ctx", "head"), None, None)
    return jax.shard_map(shards, mesh=mesh, in_specs=in_specs, out_specs=out_specs, check_vma=False)
```

time: 309 us -> 262 us (0.85)
  starting transfers between devices: 48.9 us -> 22.7 us
  waiting for transfers between devices: 65.7 us -> 41.8 us
  blocking collectives: 102 us -> 123 us
  Pallas kernels: 76.5 us -> 57.1 us
    all_to_all x3 -> x4, starting transfers between devices: 48.9 us -> 22.7 us  [exchange(): lax.all_to_all(x, 'ctx', split_axis=0, concat_axis=0, tiled=True, axis_in...]
    all_to_all x3 -> x4, waiting for transfers between devices: 65.7 us -> 41.8 us  [exchange(): lax.all_to_all(x, 'ctx', split_axis=0, concat_axis=0, tiled=True, axis_in...]
    all_to_all x3 -> x2, blocking collectives: 74.9 us -> 94.6 us  [exchange(): lax.all_to_all(x, 'ctx', split_axis=0, concat_axis=0, tiled=True, axis_in...]
    pallas_call x6, Pallas kernels: 68 us -> 48.6 us  [the longest x2 27.2 us: block_part(): pl.pallas_call(functools.partial(block_kernel, factor, groups, capacity),...]
    unnamed x13 -> x17, local copies, waits for them, and re-layouts: 8.1 us -> 7.4 us
  transfers between devices with their start and end apart: 3 -> 4, of which waited for: 3 -> 3; matrix products, arithmetic and copies ran while one was open for 2% -> 2% of each run, Pallas kernels for 5% -> 16%
where the time goes in v4:
time: 262 us; the launch traced here: 260 us
  blocking collectives  123 us (47%)
  Pallas kernels  57.1 us (22%)
  waiting for transfers between devices  41.8 us (16%)
  starting transfers between devices  22.7 us (9%)
  local copies, waits for them, and re-layouts  12.1 us (5%)
    all_to_all x2, blocking collectives, exchange(): lax.all_to_all(x, 'ctx', split_axis=0, concat_axis=0, tiled=True, axis_in...  94.6 us
    all_to_all x4, waiting for transfers between devices, exchange(): lax.all_to_all(x, 'ctx', split_axis=0, concat_axis=0, tiled=True, axis_in...  41.8 us
    pallas_call x2, Pallas kernels, block_part(): pl.pallas_call(functools.partial(block_kernel, factor, groups, capacity),...  27.2 us
    all_to_all x4, starting transfers between devices, exchange(): lax.all_to_all(x, 'ctx', split_axis=0, concat_axis=0, tiled=True, axis_in...  22.7 us
    all_to_all x1, blocking collectives, shards(): lax.all_to_all(result, 'head', split_axis=0, concat_axis=0, tiled=True)  14.5 us
    all_to_all x1, blocking collectives, shards(): lax.all_to_all(mixed, 'head', split_axis=0, concat_axis=0, tiled=True)  14.2 us
    pallas_call x1, Pallas kernels, column_part(): pl.pallas_call(functools.partial(column_kernel, groups), out_shape=jax.Sh...  8.84 us
    pallas_call x1, Pallas kernels, fresh_part(): pl.pallas_call(functools.partial(fresh_kernel, factor, ring, tokens), out...  8.44 us
  transfers between devices with their start and end apart: 4, of which 3 were waited for; matrix products, arithmetic and copies ran while one was open for 2% of the time, Pallas kernels for 16%

profile of v4, /device:TPU:1, one launch (start us, length us, event | category | flops | bytes accessed | tf_op | source)
XLA Modules:
  0.0 260.3 jit_solution(2206249092433370232)
XLA Ops:
  0.0 0.9 copy.27
  0.9 0.7 copy_bitcast_fusion.3
  1.6 14.2 %all_to_all.50 = bf16[8,6,8,128]{3,2,1,0:T(8,128)(2,1)S(1)} all-to-all(bf16[8,6,8,128]{3,2,1,0:T(8,128)(2,1)S(1)} %maximum_bitcast_fusion), channel_id=1, replica_groups=mesh['ctx'=64,'head'=8] {'head'}, dimensions={0} | all-to-all | bytes 196608 | tf_op jit(solution)/shard_map/all_to_all | solution.py:469
  15.9 0.0 copy-start.6
  15.9 1.2 broadcast_in_dim.16
  17.1 11.3 %all-to-all-start.3 = ((bf16[16,256,128]{2,1,0:T(8,128)(2,1)}), bf16[16,256,128]{2,1,0:T(8,128)(2,1)S(1)}, u32[]{:S(2)}, u32[]{:S(2)}) async-start(bf16[16,256,128]{2,1,0:T(8,128)(2,1)} %broadcast_in_dim.16), calls=%async_computation.3 | async-start | bytes 2097152 | tf_op jit(solution)/shard_map/all_to_all | solution.py:473
  28.4 0.0 copy-done.6
  28.4 0.7 copy.26.sel_ref
  29.1 7.1 %plan.1 = (s32[6]{0:T(128)}, s32[32]{0:T(128)}, s32[1]{0:T(128)}, s32[1]{0:T(128)}) custom-call(s32[1]{0:T(128)} %bitcast.me_ref, s32[32,12]{1,0:T(8,128)} %copy.26.sel_ref), custom_call_target="tpu_custom_call" | custom-call | tf_op jit(solution)/shard_map/plan/pallas_call | solution.py:71
  36.2 0.6 slice.23
  36.8 36.3 %all-to-all-done.3 = bf16[16,256,128]{2,1,0:T(8,128)(2,1)S(1)} async-done(((bf16[16,256,128]{2,1,0:T(8,128)(2,1)}), bf16[16,256,128]{2,1,0:T(8,128)(2,1)S(1)}, u32[]{:S(2)}, u32[]{:S(2)}) %all-to-all-start.3) | async-done | bytes 1048608 | tf_op jit(solution)/shard_map/all_to_all | solution.py:473
  73.1 0.0 copy-start.3
  73.1 1.0 copy-done.3
  74.1 2.9 %gather_tiles.1 = (bf16[4,1152,128]{2,1,0:T(8,128)(2,1)}, bf16[4,1536,128]{2,1,0:T(8,128)(2,1)}, bf16[4,512,128]{2,1,0:T(8,128)(2,1)S(1)}) custom-call(s32[32]{0:T(128)} %get-tuple-element.36.slot_ref, bf16[8,512,128]{2,1,0:T(8,128)(2,1)} %bitcast.39, bf16[128,128]{1,0:T(8,128)(2,1)} %bitcast.54), custom_call_target="tpu_custom_call" | custom-call | tf_op jit(solution)/shard_map/gather_tiles/pallas_call | solution.py:120
  77.0 14.8 %all_to_all.51.refs_0_.refs_1_ = bf16[4,1152,128]{2,1,0:T(8,128)(2,1)} all-to-all(bf16[4,1152,128]{2,1,0:T(8,128)(2,1)} %get-tuple-element.40), channel_id=1, replica_groups={{0,128,256,384},{8,136,264,392},{16,144,272,400},{24,152,280,408},{32,1..., dimensions={0} | all-to-all | bytes 2359296 | tf_op jit(solution)/shard_map/all_to_all | solution.py:473
  91.8 0.0 copy-start.5
  91.8 3.7 %all-to-all-start.5 = ((bf16[4,1536,128]{2,1,0:T(8,128)(2,1)}), bf16[4,1536,128]{2,1,0:T(8,128)(2,1)S(1)}, u32[]{:S(2)}, u32[]{:S(2)}) async-start(bf16[4,1536,128]{2,1,0:T(8,128)(2,1)} %get-tuple-element.44), calls=%async_computation.5 | async-start | bytes 3145728 | tf_op jit(solution)/shard_map/all_to_all | solution.py:473
  96.8 0.0 copy-done.5
  96.8 1.4 copy.31
  98.2 1.2 pad_add_fusion
  99.4 19.8 %block_part.2 = s16[4,2,2,264,128]{4,3,2,1,0:T(8,128)(2,1)} custom-call(s32[6]{0:T(128)} %get-tuple-element.37.place_ref, s32[2]{0:T(128)} %get-tuple-element.59.span_ref, s32[1]{0:T(128)S(6)} %min.6.valid_ref, bf16[4,1152,128]{2,1,0:T(8,128)(2,1)} %all_to_all.51.refs_0_.refs_1_, bf16[4,1152,128]{2,1,0:T(8,128)(2,1)} %all_to_all.51.refs_0_.refs_1_, ...), custom_call_target="tpu_custom_call" | custom-call | tf_op jit(solution)/shard_map/block_part/pallas_call | solution.py:278
  119.1 0.0 all-to-all-done.5.refs_0_.refs_2_
  119.2 0.0 copy-start.2
  119.2 0.0 copy-start.4
  119.2 0.9 copy-done.4
  120.1 0.4 copy-done.2
  120.5 4.2 %all-to-all-start.6 = ((s16[4,2,2,264,128]{4,3,2,1,0:T(8,128)(2,1)}), s16[4,2,2,264,128]{4,3,2,1,0:T(8,128)(2,1)S(1)}, u32[]{:S(2)}, u32[]{:S(2)}) async-start(s16[4,2,2,264,128]{4,3,2,1,0:T(8,128)(2,1)} %block_part.2), calls=%async_computation.6 | async-start | bytes 2162688 | tf_op jit(solution)/shard_map/all_to_all | solution.py:473
  124.7 7.5 %block_part.3 = (s16[4,3,2,264,128]{4,3,2,1,0:T(8,128)(2,1)}, s16[4,1,2,264,128]{4,3,2,1,0:T(8,128)(2,1)S(1)}) custom-call(s32[6]{0:T(128)} %get-tuple-element.37.place_ref, s32[2]{0:T(128)} %get-tuple-element.42.span_ref, s32[1]{0:T(128)S(6)} %min.6.valid_ref, bf16[4,1536,128]{2,1,0:T(8,128)(2,1)} %copy-done.2, bf16[4,512,128]{2,1,0:T(8,128)(2,1)} %copy-done.4, ...), custom_call_target="tpu_custom_call" | custom-call | tf_op jit(solution)/shard_map/block_part/pallas_call | solution.py:278
  132.2 2.5 all-to-all-done.6.refs_0_.refs_3_.refs_6_.refs_9_
  134.6 0.0 copy-start.1
  134.6 0.0 slice-start
  134.6 1.0 copy-done.1
  135.6 3.6 %all-to-all-start.7 = ((s16[4,3,2,264,128]{4,3,2,1,0:T(8,128)(2,1)}), s16[4,3,2,264,128]{4,3,2,1,0:T(8,128)(2,1)S(1)}, u32[]{:S(2)}, u32[]{:S(2)}) async-start(s16[4,3,2,264,128]{4,3,2,1,0:T(8,128)(2,1)} %get-tuple-element.52), calls=%async_computation.7 | async-start | bytes 3244032 | tf_op jit(solution)/shard_map/all_to_all | solution.py:473
  139.2 0.6 pad_add_fusion.2.me_ref
  139.8 0.0 slice-done
  139.8 0.7 fusion
  140.5 8.4 %fresh_part.1 = (f32[8,2,256,128]{3,2,1,0:T(8,128)}, f32[8,2,256,128]{3,2,1,0:T(8,128)}) custom-call(s32[2]{0:T(128)} %pad_add_fusion.2.me_ref, bf16[8,2,256,128]{3,2,1,0:T(8,128)(2,1)} %bitcast.40, bf16[256,128]{1,0:T(8,128)(2,1)} %bitcast.51, bf16[256,128]{1,0:T(8,128)(2,1)} %bitcast.50), custom_call_target="tpu_custom_call" | custom-call | tf_op jit(solution)/shard_map/fresh_part/pallas_call | solution.py:336
  148.9 3.1 %all-to-all-done.7.refs_1_.refs_4_.refs_7_.refs_10_ = s16[4,3,2,264,128]{4,3,2,1,0:T(8,128)(2,1)S(1)} async-done(((s16[4,3,2,264,128]{4,3,2,1,0:T(8,128)(2,1)}), s16[4,3,2,264,128]{4,3,2,1,0:T(8,128)(2,1)S(1)}, u32[]{:S(2)}, u32[]{:S(2)}) %all-to-all-start.7) | async-done | bytes 1622048 | tf_op jit(solution)/shard_map/all_to_all | solution.py:473
  152.0 0.0 copy-start
  152.0 1.2 copy-done
  153.2 8.8 %column_part.1 = s16[16,264,128]{2,1,0:T(8,128)(2,1)} custom-call(s32[32]{0:T(128)} %get-tuple-element.36.slot_ref, s16[4,2,2,264,128]{4,3,2,1,0:T(8,128)(2,1)} %copy-done.1, s16[4,3,2,264,128]{4,3,2,1,0:T(8,128)(2,1)} %copy-done, s16[4,1,2,264,128]{4,3,2,1,0:T(8,128)(2,1)S(1)} %get-tuple-element.64.refs_2_.refs_5_.refs_8_.refs_11_, ...), custom_call_target="tpu_custom_call" | custom-call | tf_op jit(solution)/shard_map/column_part/pallas_call | solution.py:403
  162.0 79.8 %all_to_all.52.got_ref = s16[16,264,128]{2,1,0:T(8,128)(2,1)} all-to-all(s16[16,264,128]{2,1,0:T(8,128)(2,1)} %column_part.1), channel_id=1, replica_groups={{0,8,16,24,32,40,48,56,64,72,80,88,96,104,112,120},{128,136,144,152,160..., dimensions={0} | all-to-all | bytes 2162688 | tf_op jit(solution)/shard_map/all_to_all | solution.py:473
  241.8 2.5 ring_part.1
  244.3 0.9 copy.45
  245.2 14.5 %all_to_all.53 = bf16[8,4,8,128]{3,2,1,0:T(8,128)(2,1)S(1)} all-to-all(bf16[8,4,8,128]{3,2,1,0:T(8,128)(2,1)S(1)} %bitcast.52), channel_id=1, replica_groups=mesh['ctx'=64,'head'=8] {'head'}, dimensions={0} | all-to-all | bytes 131072 | tf_op jit(solution)/shard_map/all_to_all | solution.py:526
  259.7 0.6 copy.44
  (5 shorter events, 0.0 us)
Async XLA Ops:
  15.9 12.5 %copy-start.6 = (s32[32,12]{0,1:T(8,128)S(1)}, s32[32,12]{0,1:T(8,128)}, u32[]{:S(2)}) copy-start(s32[32,12]{0,1:T(8,128)} %param.16) | copy-start | bytes 4612
  17.1 56.0 %all-to-all-start.3 = ((bf16[16,256,128]{2,1,0:T(8,128)(2,1)}), bf16[16,256,128]{2,1,0:T(8,128)(2,1)S(1)}, u32[]{:S(2)}, u32[]{:S(2)}) async-start(bf16[16,256,128]{2,1,0:T(8,128)(2,1)} %broadcast_in_dim.16), calls=%async_computation.3 | async-start | bytes 2097152 | tf_op jit(solution)/shard_map/all_to_all | solution.py:473
  73.1 1.0 copy-start.3
  91.8 5.0 %copy-start.5 = (bf16[4096,1,128]{2,0,1:T(8,128)(2,1)S(1)}, bf16[4096,1,128]{2,0,1:T(8,128)(2,1)}, u32[]{:S(2)}) copy-start(bf16[4096,1,128]{2,0,1:T(8,128)(2,1)} %param.14) | copy-start | bytes 3145732
  91.8 27.4 %all-to-all-start.5 = ((bf16[4,1536,128]{2,1,0:T(8,128)(2,1)}), bf16[4,1536,128]{2,1,0:T(8,128)(2,1)S(1)}, u32[]{:S(2)}, u32[]{:S(2)}) async-start(bf16[4,1536,128]{2,1,0:T(8,128)(2,1)} %get-tuple-element.44), calls=%async_computation.5 | async-start | bytes 3145728 | tf_op jit(solution)/shard_map/all_to_all | solution.py:473
  119.2 1.3 copy-start.2
  119.2 0.9 copy-start.4
  120.5 14.1 %all-to-all-start.6 = ((s16[4,2,2,264,128]{4,3,2,1,0:T(8,128)(2,1)}), s16[4,2,2,264,128]{4,3,2,1,0:T(8,128)(2,1)S(1)}, u32[]{:S(2)}, u32[]{:S(2)}) async-start(s16[4,2,2,264,128]{4,3,2,1,0:T(8,128)(2,1)} %block_part.2), calls=%async_computation.6 | async-start | bytes 2162688 | tf_op jit(solution)/shard_map/all_to_all | solution.py:473
  134.6 1.0 copy-start.1
  134.6 5.2 %slice-start = ((bf16[4,1152,128]{2,1,0:T(8,128)(2,1)}), bf16[4,128,128]{2,1,0:T(8,128)(2,1)S(1)}, s32[]{:S(2)}) async-start(bf16[4,1152,128]{2,1,0:T(8,128)(2,1)} %all_to_all.51.refs_0_.refs_1_), calls=%async_computation.10 | async-start | bytes 262144 | tf_op jit(solution)/shard_map/slice | solution.py:506
  135.6 16.4 %all-to-all-start.7 = ((s16[4,3,2,264,128]{4,3,2,1,0:T(8,128)(2,1)}), s16[4,3,2,264,128]{4,3,2,1,0:T(8,128)(2,1)S(1)}, u32[]{:S(2)}, u32[]{:S(2)}) async-start(s16[4,3,2,264,128]{4,3,2,1,0:T(8,128)(2,1)} %get-tuple-element.52), calls=%async_computation.7 | async-start | bytes 3244032 | tf_op jit(solution)/shard_map/all_to_all | solution.py:473
  152.0 1.2 copy-start

commit v5 on v4

--- a/solution.py
+++ b/solution.py
@@ -474,9 +474,6 @@
             x, "ctx", split_axis=0, concat_axis=0, tiled=True, axis_index_groups=groups
         )
 
-    def copies(x, n):
-        return jnp.broadcast_to(x[None], (n,) + x.shape)
-
     me = jnp.stack([ctx_index // ring, ctx_index % ring])
     kt = cache_keys[:, 0].T
     v = cache_values[:, 0]
@@ -495,7 +492,9 @@
             return lax.cond(over[0] > 0, lambda a: exchange(a, across), lambda a: a, x), after
         return exchange(x, across), after
 
-    q = exchange(copies(mixed[:group].reshape(rows, head_size), ring), along)
+    q = lax.all_gather(
+        mixed[:group].reshape(rows, head_size), "ctx", axis=0, tiled=True, axis_index_groups=along
+    )
     q = q.reshape(per_row, full, head_size)
     first, second, third = gather_tiles(
         groups, slot, q, mixed[group:].reshape(2 * tokens, head_size), columns

time: 262 us -> 266 us (1.015)
  waiting for transfers between devices: 41.8 us -> 61.8 us
  blocking collectives: 123 us -> 104 us
  between operations: 1.46 us -> 14.9 us
  starting transfers between devices: 22.7 us -> 11.5 us
    all_gather x0 -> x1, waiting for transfers between devices: none -> 50.5 us  [shards(): lax.all_gather(mixed[:group].reshape(rows, head_size), 'ctx', axis=0, til...]
    all_to_all x2, blocking collectives: 94.6 us -> 60.9 us  [exchange(): lax.all_to_all(x, 'ctx', split_axis=0, concat_axis=0, tiled=True, axis_in...]
    all_to_all x4 -> x3, waiting for transfers between devices: 41.8 us -> 11.3 us  [exchange(): lax.all_to_all(x, 'ctx', split_axis=0, concat_axis=0, tiled=True, axis_in...]
    all_to_all x1, blocking collectives: 14.5 us -> 28.6 us  [shards(): lax.all_to_all(result, 'head', split_axis=0, concat_axis=0, tiled=True)]
    all_to_all x4 -> x3, starting transfers between devices: 22.7 us -> 11.5 us  [exchange(): lax.all_to_all(x, 'ctx', split_axis=0, concat_axis=0, tiled=True, axis_in...]
    unnamed x17 -> x13, local copies, waits for them, and re-layouts: 7.4 us -> 7.07 us
where the time goes in v5:
time: 266 us; the launch traced here: 265 us
  blocking collectives  104 us (39%)
  waiting for transfers between devices  61.8 us (23%)
  Pallas kernels  59.6 us (22%)
  between operations  14.9 us (6%)
  starting transfers between devices  11.5 us (4%)
  local copies, waits for them, and re-layouts  11.2 us (4%)
    all_to_all x2, blocking collectives, exchange(): lax.all_to_all(x, 'ctx', split_axis=0, concat_axis=0, tiled=True, axis_in...  60.9 us
    all_gather x1, waiting for transfers between devices, shards(): lax.all_gather(mixed[:group].reshape(rows, head_size), 'ctx', axis=0, til...  50.5 us
    all_to_all x1, blocking collectives, shards(): lax.all_to_all(result, 'head', split_axis=0, concat_axis=0, tiled=True)  28.6 us
    pallas_call x2, Pallas kernels, block_part(): pl.pallas_call(functools.partial(block_kernel, factor, groups, capacity),...  27.3 us
    all_to_all x1, blocking collectives, shards(): lax.all_to_all(mixed, 'head', split_axis=0, concat_axis=0, tiled=True)  14.2 us
    all_to_all x3, starting transfers between devices, exchange(): lax.all_to_all(x, 'ctx', split_axis=0, concat_axis=0, tiled=True, axis_in...  11.5 us
    all_to_all x3, waiting for transfers between devices, exchange(): lax.all_to_all(x, 'ctx', split_axis=0, concat_axis=0, tiled=True, axis_in...  11.3 us
    pallas_call x1, Pallas kernels, column_part(): pl.pallas_call(functools.partial(column_kernel, groups), out_shape=jax.Sh...  11.3 us
  transfers between devices with their start and end apart: 4, of which 3 were waited for; matrix products, arithmetic and copies ran while one was open for 2% of the time, Pallas kernels for 16%

profile of v5, /device:TPU:1, one launch (start us, length us, event | category | flops | bytes accessed | tf_op | source)
XLA Modules:
  0.0 264.6 jit_solution(13167814452327781283)
XLA Ops:
  6.5 0.0 all-gather.2.cloned.1.call-start
  6.5 0.9 copy.27
  7.4 0.7 copy_bitcast_fusion.3
  8.2 14.2 %all_to_all.45 = bf16[8,6,8,128]{3,2,1,0:T(8,128)(2,1)S(1)} all-to-all(bf16[8,6,8,128]{3,2,1,0:T(8,128)(2,1)S(1)} %maximum_bitcast_fusion), channel_id=1, replica_groups=mesh['ctx'=64,'head'=8] {'head'}, dimensions={0} | all-to-all | bytes 196608 | tf_op jit(solution)/shard_map/all_to_all | solution.py:469
  22.4 0.6 slice.22
  23.0 0.0 all-gather.2.cloned.1.call-update
  23.1 1.4 copy.26.sel_ref
  24.4 7.1 %plan.1 = (s32[6]{0:T(128)}, s32[32]{0:T(128)}, s32[1]{0:T(128)}, s32[1]{0:T(128)}) custom-call(s32[1]{0:T(128)} %bitcast.me_ref, s32[32,12]{1,0:T(8,128)} %copy.26.sel_ref), custom_call_target="tpu_custom_call" | custom-call | tf_op jit(solution)/shard_map/plan/pallas_call | solution.py:71
  31.6 0.6 slice.23
  32.2 50.5 %all-gather.2.cloned.1.call-done = bf16[4096,128]{1,0:T(8,128)(2,1)} async-done(((bf16[256,128]{1,0:T(8,128)(2,1)}), bf16[4096,128]{1,0:T(8,128)(2,1)}) %all-gather.2.cloned.1.call-update) | async-done | bytes 1048592 | tf_op jit(solution)/shard_map/all_gather | solution.py:495
  82.7 2.9 %gather_tiles.1 = (bf16[4,1152,128]{2,1,0:T(8,128)(2,1)}, bf16[4,1536,128]{2,1,0:T(8,128)(2,1)}, bf16[4,512,128]{2,1,0:T(8,128)(2,1)S(1)}) custom-call(s32[32]{0:T(128)} %get-tuple-element.36.slot_ref, bf16[8,512,128]{2,1,0:T(8,128)(2,1)} %bitcast.43, bf16[128,128]{1,0:T(8,128)(2,1)} %bitcast.54), custom_call_target="tpu_custom_call" | custom-call | tf_op jit(solution)/shard_map/gather_tiles/pallas_call | solution.py:120
  85.6 14.8 %all_to_all.46.refs_0_.refs_1_ = bf16[4,1152,128]{2,1,0:T(8,128)(2,1)} all-to-all(bf16[4,1152,128]{2,1,0:T(8,128)(2,1)} %get-tuple-element.40), channel_id=1, replica_groups={{0,128,256,384},{8,136,264,392},{16,144,272,400},{24,152,280,408},{32,1..., dimensions={0} | all-to-all | bytes 2359296 | tf_op jit(solution)/shard_map/all_to_all | solution.py:473
  100.4 0.0 copy-start.4
  100.4 3.7 %all-to-all-start.4 = ((bf16[4,1536,128]{2,1,0:T(8,128)(2,1)}), bf16[4,1536,128]{2,1,0:T(8,128)(2,1)S(1)}, u32[]{:S(2)}, u32[]{:S(2)}) async-start(bf16[4,1536,128]{2,1,0:T(8,128)(2,1)} %get-tuple-element.44), calls=%async_computation.4 | async-start | bytes 3145728 | tf_op jit(solution)/shard_map/all_to_all | solution.py:473
  105.5 0.0 copy-done.4
  105.5 1.3 copy.31
  106.8 1.3 pad_add_fusion
  108.1 19.8 %block_part.2 = s16[4,2,2,264,128]{4,3,2,1,0:T(8,128)(2,1)} custom-call(s32[6]{0:T(128)} %get-tuple-element.37.place_ref, s32[2]{0:T(128)} %get-tuple-element.59.span_ref, s32[1]{0:T(128)S(6)} %min.6.valid_ref, bf16[4,1152,128]{2,1,0:T(8,128)(2,1)} %all_to_all.46.refs_0_.refs_1_, bf16[4,1152,128]{2,1,0:T(8,128)(2,1)} %all_to_all.46.refs_0_.refs_1_, ...), custom_call_target="tpu_custom_call" | custom-call | tf_op jit(solution)/shard_map/block_part/pallas_call | solution.py:278
  127.9 0.0 all-to-all-done.4.refs_0_.refs_2_
  127.9 0.0 copy-start.2
  127.9 0.0 copy-start.3
  127.9 0.9 copy-done.3
  128.8 0.4 copy-done.2
  129.2 4.2 %all-to-all-start.5 = ((s16[4,2,2,264,128]{4,3,2,1,0:T(8,128)(2,1)}), s16[4,2,2,264,128]{4,3,2,1,0:T(8,128)(2,1)S(1)}, u32[]{:S(2)}, u32[]{:S(2)}) async-start(s16[4,2,2,264,128]{4,3,2,1,0:T(8,128)(2,1)} %block_part.2), calls=%async_computation.5 | async-start | bytes 2162688 | tf_op jit(solution)/shard_map/all_to_all | solution.py:473
  133.4 7.5 %block_part.3 = (s16[4,3,2,264,128]{4,3,2,1,0:T(8,128)(2,1)}, s16[4,1,2,264,128]{4,3,2,1,0:T(8,128)(2,1)S(1)}) custom-call(s32[6]{0:T(128)} %get-tuple-element.37.place_ref, s32[2]{0:T(128)} %get-tuple-element.42.span_ref, s32[1]{0:T(128)S(6)} %min.6.valid_ref, bf16[4,1536,128]{2,1,0:T(8,128)(2,1)} %copy-done.2, bf16[4,512,128]{2,1,0:T(8,128)(2,1)} %copy-done.3, ...), custom_call_target="tpu_custom_call" | custom-call | tf_op jit(solution)/shard_map/block_part/pallas_call | solution.py:278
  140.9 2.4 all-to-all-done.5.refs_0_.refs_3_.refs_6_.refs_9_
  143.3 0.0 copy-start.1
  143.3 0.0 slice-start
  143.3 1.0 copy-done.1
  144.3 3.6 %all-to-all-start.6 = ((s16[4,3,2,264,128]{4,3,2,1,0:T(8,128)(2,1)}), s16[4,3,2,264,128]{4,3,2,1,0:T(8,128)(2,1)S(1)}, u32[]{:S(2)}, u32[]{:S(2)}) async-start(s16[4,3,2,264,128]{4,3,2,1,0:T(8,128)(2,1)} %get-tuple-element.52), calls=%async_computation.6 | async-start | bytes 3244032 | tf_op jit(solution)/shard_map/all_to_all | solution.py:473
  147.9 0.6 pad_add_fusion.2.me_ref
  148.5 0.0 slice-done
  148.5 0.7 fusion
  149.2 8.4 %fresh_part.1 = (f32[8,2,256,128]{3,2,1,0:T(8,128)}, f32[8,2,256,128]{3,2,1,0:T(8,128)}) custom-call(s32[2]{0:T(128)} %pad_add_fusion.2.me_ref, bf16[8,2,256,128]{3,2,1,0:T(8,128)(2,1)} %bitcast.44, bf16[256,128]{1,0:T(8,128)(2,1)} %bitcast.51, bf16[256,128]{1,0:T(8,128)(2,1)} %bitcast.50), custom_call_target="tpu_custom_call" | custom-call | tf_op jit(solution)/shard_map/fresh_part/pallas_call | solution.py:336
  157.6 8.9 %all-to-all-done.6.refs_1_.refs_4_.refs_7_.refs_10_ = s16[4,3,2,264,128]{4,3,2,1,0:T(8,128)(2,1)S(1)} async-done(((s16[4,3,2,264,128]{4,3,2,1,0:T(8,128)(2,1)}), s16[4,3,2,264,128]{4,3,2,1,0:T(8,128)(2,1)S(1)}, u32[]{:S(2)}, u32[]{:S(2)}) %all-to-all-start.6) | async-done | bytes 1622048 | tf_op jit(solution)/shard_map/all_to_all | solution.py:473
  166.5 0.0 copy-start
  166.5 1.2 copy-done
  167.7 11.3 %column_part.1 = s16[16,264,128]{2,1,0:T(8,128)(2,1)} custom-call(s32[32]{0:T(128)} %get-tuple-element.36.slot_ref, s16[4,2,2,264,128]{4,3,2,1,0:T(8,128)(2,1)} %copy-done.1, s16[4,3,2,264,128]{4,3,2,1,0:T(8,128)(2,1)} %copy-done, s16[4,1,2,264,128]{4,3,2,1,0:T(8,128)(2,1)S(1)} %get-tuple-element.64.refs_2_.refs_5_.refs_8_.refs_11_, ...), custom_call_target="tpu_custom_call" | custom-call | tf_op jit(solution)/shard_map/column_part/pallas_call | solution.py:403
  179.0 46.1 %all_to_all.47.got_ref = s16[16,264,128]{2,1,0:T(8,128)(2,1)} all-to-all(s16[16,264,128]{2,1,0:T(8,128)(2,1)} %column_part.1), channel_id=1, replica_groups={{0,8,16,24,32,40,48,56,64,72,80,88,96,104,112,120},{128,136,144,152,160..., dimensions={0} | all-to-all | bytes 2162688 | tf_op jit(solution)/shard_map/all_to_all | solution.py:473
  225.1 2.5 ring_part.1
  227.7 0.9 copy.45
  228.5 28.6 %all_to_all.48 = bf16[8,4,8,128]{3,2,1,0:T(8,128)(2,1)S(1)} all-to-all(bf16[8,4,8,128]{3,2,1,0:T(8,128)(2,1)S(1)} %bitcast.52), channel_id=1, replica_groups=mesh['ctx'=64,'head'=8] {'head'}, dimensions={0} | all-to-all | bytes 131072 | tf_op jit(solution)/shard_map/all_to_all | solution.py:525
  257.1 0.6 copy.44
  (4 shorter events, 0.0 us)
Async XLA Ops:
  6.5 76.1 %all-gather.2.cloned.1.call-start = ((), (), s32[]{:S(2)}) async-start(), calls=%async_computation.9 | async-start | bytes 1114112 | tf_op jit(solution)/shard_map/all_gather | solution.py:495
  100.4 5.0 %copy-start.4 = (bf16[4096,1,128]{2,0,1:T(8,128)(2,1)S(1)}, bf16[4096,1,128]{2,0,1:T(8,128)(2,1)}, u32[]{:S(2)}) copy-start(bf16[4096,1,128]{2,0,1:T(8,128)(2,1)} %param.14) | copy-start | bytes 3145732
  100.4 27.4 %all-to-all-start.4 = ((bf16[4,1536,128]{2,1,0:T(8,128)(2,1)}), bf16[4,1536,128]{2,1,0:T(8,128)(2,1)S(1)}, u32[]{:S(2)}, u32[]{:S(2)}) async-start(bf16[4,1536,128]{2,1,0:T(8,128)(2,1)} %get-tuple-element.44), calls=%async_computation.4 | async-start | bytes 3145728 | tf_op jit(solution)/shard_map/all_to_all | solution.py:473
  127.9 1.3 copy-start.2
  127.9 0.9 copy-start.3
  129.2 14.1 %all-to-all-start.5 = ((s16[4,2,2,264,128]{4,3,2,1,0:T(8,128)(2,1)}), s16[4,2,2,264,128]{4,3,2,1,0:T(8,128)(2,1)S(1)}, u32[]{:S(2)}, u32[]{:S(2)}) async-start(s16[4,2,2,264,128]{4,3,2,1,0:T(8,128)(2,1)} %block_part.2), calls=%async_computation.5 | async-start | bytes 2162688 | tf_op jit(solution)/shard_map/all_to_all | solution.py:473
  143.3 1.0 copy-start.1
  143.3 5.2 %slice-start = ((bf16[4,1152,128]{2,1,0:T(8,128)(2,1)}), bf16[4,128,128]{2,1,0:T(8,128)(2,1)S(1)}, s32[]{:S(2)}) async-start(bf16[4,1152,128]{2,1,0:T(8,128)(2,1)} %all_to_all.46.refs_0_.refs_1_), calls=%async_computation.10 | async-start | bytes 262144 | tf_op jit(solution)/shard_map/slice | solution.py:505
  144.3 22.1 %all-to-all-start.6 = ((s16[4,3,2,264,128]{4,3,2,1,0:T(8,128)(2,1)}), s16[4,3,2,264,128]{4,3,2,1,0:T(8,128)(2,1)S(1)}, u32[]{:S(2)}, u32[]{:S(2)}) async-start(s16[4,3,2,264,128]{4,3,2,1,0:T(8,128)(2,1)} %get-tuple-element.52), calls=%async_computation.6 | async-start | bytes 3244032 | tf_op jit(solution)/shard_map/all_to_all | solution.py:473
  166.5 1.2 copy-start
Sparse Core Ops, SparseCore 0:
  23.2 59.4 all-gather.1
